TPU v7x, 512 devices: a whole 4x4x16 slice. The times are simulated.
512 devices in a mesh: bead: 64 (over z, y), slab: 8 (over x, core).
Axes of the slice: x: 4, y: 4, z: 16, core: 2. Of those that a mesh axis runs over, the one named last changes fastest.
Arguments:
- positions: float32 [3, 64, 1024], P(None, 'bead', 'slab'), may hold values from -5 to 5
- velocities: float32 [3, 64, 1024], P(None, 'bead', 'slab'), may hold values from -5 to 5
- atom_types: int32 [1024], P('slab'), may hold values from 0 to 1
- live_atoms: int32 [8], P('slab'), may hold values from 16 to 128, as said below
- halo_rows: int32 [8, 128], P('slab'), may hold values from 0 to 127, as said below
- neighbours: int32 [1024, 128], P('slab'), may hold values from -1 to 255, as said below
- type_scale: float32 [2, 25], replicated, may hold values from -4 to 4
- type_shift: float32 [2, 25], replicated, may hold values from -4 to 4
- embed_two: bfloat16 [25, 50], replicated, may hold values from -1.25 to 1.25
- embed_bias_two: float32 [50], replicated, may hold values from -3 to 3
- embed_three: bfloat16 [50, 100], replicated, may hold values from -0.875 to 0.875
- embed_bias_three: float32 [100], replicated, may hold values from -3 to 3
- fit_first: bfloat16 [1600, 240], replicated, may hold values from -0.625 to 0.625
- fit_bias_first: float32 [240], replicated, may hold values from -3 to 3
- fit_second: bfloat16 [240, 240], replicated, may hold values from -0.375 to 0.375
- fit_bias_second: float32 [240], replicated, may hold values from -3 to 3
- fit_third: bfloat16 [240, 240], replicated, may hold values from -0.375 to 0.375
- fit_bias_third: float32 [240], replicated, may hold values from -3 to 3
- fit_readout: float32 [2, 240], replicated, may hold values from -0.375 to 0.375
Outputs:
- positions_new: float32 [3, 64, 1024], P(None, 'bead', 'slab')
- velocities_new: float32 [3, 64, 1024], P(None, 'bead', 'slab')
- forces: float32 [3, 64, 1024], P(None, 'bead', 'slab')
Inputs may be any that keep to these rules, and one draw needn't show every extreme that they name: Slab s holds atoms in its first live_atoms[s] rows; one slab is full. The system is a water film with vacuum on both sides, so slabs crossing the vacuum hold few atoms. `halo_rows`: each entry is an occupied row of its slab; the first 64 of a slab go to the slab one lower (cyclic), the other 64 to the slab one higher. `neighbours`: -1 marks an empty slot; entries below 128 are occupied own rows of the slab, never the atom itself; entries from 128 on index the extended list's halo part. Rows at or past a slab's live count are all empty; an occupied row has between 64 and 128 filled slots, first, and some row of each slab has 128.
All inputs are finite; a program needn't handle non-finite values.
Results may differ from a plain program's by a relative error of at most 0.014.
Values sent between devices are 32-bit elements; how exact they have to be, the bound alone decides.
A program may use at most 64 MiB of HBM per device.

v0:
```python
import jax
import jax.numpy as jnp
from jax import lax
from jax.sharding import PartitionSpec as P

M2 = 16
BLOCK = 32


step_size = 0.25
phase_rate = 1.2
cutoff_sq = 16.0
softening = 0.25
heavy_mass = 16.0


def padded_2(cells, sides, width):
    for axis, dim in sides:
        count = lax.axis_size(axis)
        head = lax.slice_in_dim(cells, 0, width, axis=dim)
        tail = lax.slice_in_dim(cells, cells.shape[dim] - width, cells.shape[dim], axis=dim)
        cells = jnp.concatenate(
            [
                lax.ppermute(tail, axis, [(i, (i + 1) % count) for i in range(count)]),
                cells,
                lax.ppermute(head, axis, [((i + 1) % count, i) for i in range(count)]),
            ],
            axis=dim,
        )
    return cells


def in_blocks(x, dim, peers):
    dims = x.shape
    pieces = x.reshape(*dims[:dim], peers, dims[dim] // peers, *dims[dim + 1 :])
    return jnp.moveaxis(pieces, dim, 0)


def sum_at_owner(x, axis, dim):
    pieces = in_blocks(x, dim, lax.axis_size(axis))
    arrived = lax.all_to_all(pieces, axis, split_axis=0, concat_axis=0, tiled=True)
    return arrived.sum(axis=0)


def mode_tables(bead_count):
    indices = jnp.arange(bead_count)
    bead_rows = indices[:, None].astype(jnp.float32)
    mode_cols = indices[None, :]
    mode_float = mode_cols.astype(jnp.float32)
    angles = 2.0 * jnp.pi * bead_rows * mode_float / bead_count
    norm_scale = jnp.sqrt(2.0 / bead_count)
    middle = bead_count // 2
    edge_value = 1.0 / jnp.sqrt(1.0 * bead_count)
    mode_basis = jnp.where(
        mode_cols == 0,
        edge_value,
        jnp.where(
            mode_cols < middle,
            norm_scale * jnp.cos(angles),
            jnp.where(
                mode_cols == middle,
                jnp.cos(jnp.pi * bead_rows) * edge_value,
                norm_scale * jnp.sin(angles),
            ),
        ),
    )
    sine_part = jnp.sin(jnp.pi * indices.astype(jnp.float32) / bead_count)
    ratio = 2.0 * sine_part
    phases = phase_rate * bead_count * sine_part
    guarded = jnp.where(indices == 0, 1.0, ratio)
    cosine = jnp.cos(phases)
    travel = jnp.where(indices == 0, 1.0, jnp.sin(phases) / guarded)
    spring = ratio * jnp.sin(phases)
    return (mode_basis, cosine, travel, spring)


def bead_matrices(bead_count):
    mode_basis, cosine, travel, spring = mode_tables(bead_count)

    def assemble(diagonal):
        return jnp.dot(
            mode_basis * diagonal[None, :], mode_basis.T, preferred_element_type=jnp.float32
        )

    return (assemble(cosine), assemble(travel), assemble(spring))


def block_energy(centre, beside_all, around_hydrogen, filled, centre_hydrogen, living, weights):
    (
        type_scale,
        type_shift,
        embed_two,
        embed_bias_two,
        embed_three,
        embed_bias_three,
        fit_first,
        fit_bias_first,
        fit_second,
        fit_bias_second,
        fit_third,
        fit_bias_third,
        fit_readout,
    ) = weights
    offsets = beside_all - centre[:, :, None]
    dist_sq = jnp.sum(offsets * offsets, axis=0)
    softened = jnp.sqrt(dist_sq + softening)
    switch = jnp.maximum(1.0 - dist_sq / cutoff_sq, 0.0)
    strength = filled * switch * switch / softened
    environ = jnp.concatenate([strength[None], strength[None] * offsets / softened[None]], axis=0)
    block_rows, slot_count = strength.shape
    input_scale = type_scale[0] + around_hydrogen[..., None] * (type_scale[1] - type_scale[0])
    input_shift = type_shift[0] + around_hydrogen[..., None] * (type_shift[1] - type_shift[0])
    layer_one = jnp.tanh(strength[..., None] * input_scale + input_shift).reshape(
        block_rows * slot_count, -1
    )
    layer_two = jnp.tanh(
        jnp.dot(layer_one.astype(jnp.bfloat16), embed_two, preferred_element_type=jnp.float32)
        + embed_bias_two
    )
    layer_two = layer_two + jnp.concatenate([layer_one, layer_one], axis=1)
    layer_three = jnp.tanh(
        jnp.dot(layer_two.astype(jnp.bfloat16), embed_three, preferred_element_type=jnp.float32)
        + embed_bias_three
    )
    layer_three = layer_three + jnp.concatenate([layer_two, layer_two], axis=1)
    layer_three = layer_three.reshape(block_rows, slot_count, -1)
    features = jnp.einsum("bke,cbk->bec", layer_three, environ) / slot_count
    descriptor = jnp.einsum("bec,bfc->bef", features, features[:, :M2]).reshape(block_rows, -1)
    fit_one = jnp.tanh(
        jnp.dot(descriptor.astype(jnp.bfloat16), fit_first, preferred_element_type=jnp.float32)
        + fit_bias_first
    )
    fit_two = (
        jnp.tanh(
            jnp.dot(fit_one.astype(jnp.bfloat16), fit_second, preferred_element_type=jnp.float32)
            + fit_bias_second
        )
        + fit_one
    )
    fit_three = (
        jnp.tanh(
            jnp.dot(fit_two.astype(jnp.bfloat16), fit_third, preferred_element_type=jnp.float32)
            + fit_bias_third
        )
        + fit_two
    )
    readout = fit_readout[0] + centre_hydrogen[:, None] * (fit_readout[1] - fit_readout[0])
    return jnp.sum(living * jnp.sum(fit_three * readout, axis=1))


def block_gradient(gradient, extended, wide_hydrogen, listed, first_row, living, weights):
    centre = lax.dynamic_slice_in_dim(extended, first_row, BLOCK, 1)
    filled = (listed >= 0).astype(jnp.float32)
    flat_rows = jnp.where(listed >= 0, listed, 0).reshape(-1)
    beside_all = extended[:, flat_rows].reshape(3, BLOCK, -1)
    around_hydrogen = wide_hydrogen[flat_rows].reshape(BLOCK, -1)
    centre_hydrogen = lax.dynamic_slice_in_dim(wide_hydrogen, first_row, BLOCK, 0)

    def energy_of(centre_in, around_in):
        return block_energy(
            centre_in, around_in, around_hydrogen, filled, centre_hydrogen, living, weights
        )

    energy, backward = jax.vjp(energy_of, centre, beside_all)
    grad_centre, grad_around = backward(jnp.ones_like(energy))
    gradient = gradient.at[:, flat_rows].add(grad_around.reshape(3, -1))
    current = lax.dynamic_slice_in_dim(gradient, first_row, BLOCK, 1)
    return lax.dynamic_update_slice_in_dim(gradient, current + grad_centre, first_row, 1)


def slab_gradient(extended, wide_hydrogen, slab_lists, live_count, block_count, weights):

    def add_block(block_index, gradient):
        first_row = block_index * BLOCK
        listed = lax.dynamic_slice_in_dim(slab_lists, first_row, BLOCK, 0)
        row_numbers = first_row + jnp.arange(BLOCK)
        living = (row_numbers < live_count).astype(jnp.float32)
        return block_gradient(gradient, extended, wide_hydrogen, listed, first_row, living, weights)

    zeroed = jnp.zeros(extended.shape, jnp.float32)
    return lax.fori_loop(0, block_count, add_block, zeroed)


def own_slab_force(local_field, hydrogen, live_atoms, halo_rows, neighbours, weights):
    atom_count = local_field.shape[1]
    outgoing = halo_rows[0]
    halo_half = outgoing.shape[0] // 2
    sending = jnp.concatenate([local_field[:, outgoing], hydrogen[outgoing][None]], axis=0)
    padded = padded_2(sending, (("slab", 1),), halo_half)
    extended = jnp.concatenate(
        [local_field, padded[:3, :halo_half], padded[:3, 3 * halo_half :]], axis=1
    )
    wide_hydrogen = jnp.concatenate([hydrogen, padded[3, :halo_half], padded[3, 3 * halo_half :]])
    live_count = live_atoms[0]
    block_count = (live_count + BLOCK - 1) // BLOCK
    gradient = slab_gradient(extended, wide_hydrogen, neighbours, live_count, block_count, weights)
    returned = padded_2(gradient[:, atom_count:], (("slab", 1),), halo_half)
    own_force = gradient[:, :atom_count]
    own_force = own_force.at[:, outgoing[:halo_half]].add(returned[:, :halo_half])
    own_force = own_force.at[:, outgoing[halo_half:]].add(returned[:, 3 * halo_half :])
    return -own_force


def reduce_apply(bead_field, left_matrix, right_matrix, own_bead):
    left_col = lax.dynamic_index_in_dim(left_matrix, own_bead, 1, keepdims=False)
    right_col = lax.dynamic_index_in_dim(right_matrix, own_bead, 1, keepdims=False)
    summed = sum_at_owner(
        jnp.stack(
            [
                left_col[:, None, None] * bead_field[None],
                right_col[:, None, None] * bead_field[None],
            ],
            axis=1,
        ),
        "bead",
        0,
    )
    return (summed[0, 0], summed[0, 1])


def local(
    positions,
    velocities,
    atom_types,
    live_atoms,
    halo_rows,
    neighbours,
    type_scale,
    type_shift,
    embed_two,
    embed_bias_two,
    embed_three,
    embed_bias_three,
    fit_first,
    fit_bias_first,
    fit_second,
    fit_bias_second,
    fit_third,
    fit_bias_third,
    fit_readout,
):
    weights = (
        type_scale,
        type_shift,
        embed_two,
        embed_bias_two,
        embed_three,
        embed_bias_three,
        fit_first,
        fit_bias_first,
        fit_second,
        fit_bias_second,
        fit_third,
        fit_bias_third,
        fit_readout,
    )
    hydrogen = (atom_types == 1).astype(jnp.float32)
    local_field = positions[:, 0, :]
    forces = own_slab_force(local_field, hydrogen, live_atoms, halo_rows, neighbours, weights)
    inverse_mass = jnp.where(atom_types == 1, 1.0, 1.0 / heavy_mass)
    kicked = velocities[:, 0, :] + step_size * inverse_mass[None, :] * forces
    bead_count = lax.axis_size("bead")
    own_bead = lax.axis_index("bead")
    rot_cos, rot_travel, rot_spring = bead_matrices(bead_count)
    from_positions = reduce_apply(local_field, rot_cos, -rot_spring, own_bead)
    from_velocities = reduce_apply(kicked, rot_travel, rot_cos, own_bead)
    positions_new = from_positions[0] + from_velocities[0]
    velocities_new = from_positions[1] + from_velocities[1]
    return (positions_new[:, None, :], velocities_new[:, None, :], forces[:, None, :])


def solution(mesh):
    return jax.shard_map(
        local,
        mesh=mesh,
        in_specs=(
            P(None, "bead", "slab"),
            P(None, "bead", "slab"),
            P("slab"),
            P("slab"),
            P("slab", None),
            P("slab", None),
            P(),
            P(),
            P(),
            P(),
            P(),
            P(),
            P(),
            P(),
            P(),
            P(),
            P(),
            P(),
            P(),
        ),
        out_specs=(P(None, "bead", "slab"), P(None, "bead", "slab"), P(None, "bead", "slab")),
        check_vma=False,
    )
```

profile of v0, /device:TPU:6, one launch (start us, length us, event | category | flops | bytes accessed | tf_op | source)
XLA Modules:
  0.0 473.2 jit_solution(9401116777586465452)
XLA Ops:
  2.0 0.8 copy.62
  2.8 1.2 gather_fusion.3
  5.4 1.3 fusion.131
  6.7 1.2 fusion.128
  8.9 1.3 slice_subtract_fusion
  12.2 1.1 fusion.84
  13.3 1.3 subtract_bitcast_fusion
  15.4 196.9 %while.11 = (s32[]{:T(128)}, f32[3,256]{0,1:T(8,128)S(1)}, s32[]{:T(128)}, s32[128,128]{1,0:T(8,128)}, f32[3,256]{0,1:T(8,128)S(1)}, /*index=5*/s32[]{:T(128)}, ...) while((s32[]{:T(128)}, f32[3,256]{0,1:T(8,128)S(1)}, ...), condition=%wide.region_8.9_spmd, body=%wide.region_1.8_spmd.sunk | while | flops 186988224 | bytes 41399548 | solution.py:181
  16.8 10.8 %gather_fusion = f32[4096,3]{1,0:T(8,128)S(1)} fusion(f32[3,256]{0,1:T(8,128)S(1)} %get-tuple-element.550, s32[4096]{0:T(1024)S(1)} %broadcast_clamp_fusion.2), kind=kCustom, calls=%fused_computation.clone.1 | custom fusion | bytes 114688 | tf_op jit(solution)/shard_map/while/body/gather | solution.py:155
  29.7 25.7 %gather_fusion.1 = f32[4096]{0:T(1024)S(1)} fusion(f32[256]{0:T(256)S(1)} %get-tuple-element.553, s32[4096]{0:T(1024)S(1)} %broadcast_clamp_fusion.2), kind=kCustom, calls=%fused_computation.1.clone.1 | custom fusion | bytes 49152 | tf_op jit(solution)/shard_map/while/body/gather | solution.py:156
  55.5 0.9 add_tanh_fusion.3
  56.4 2.0 maximum_add_fusion.4
  58.4 1.2 maximum_add_fusion.5
  62.3 0.9 convolution_convert_fusion.8
  63.1 2.1 copy.99
  65.2 1.4 fusion.226
  67.3 1.7 fusion.227
  69.6 1.2 slice.176
  70.8 1.2 compare_convert_fusion.3
  72.1 1.9 fusion.228
  74.0 2.1 convolution_convert_fusion.9
  76.1 1.9 copy.100
  77.9 2.1 copy.101
  80.0 1.1 fusion.229
  81.1 1.1 fusion.230
  82.6 0.9 multiply_reduce_fusion.6
  84.6 1.2 copy.103
  85.9 1.3 fusion.233
  87.3 1.2 fusion.234
  89.5 23.6 %scatter_fusion = f32[3,256]{0,1:T(8,128)S(1)} fusion(f32[3,256]{0,1:T(8,128)S(1)} %get-tuple-element.518, s32[4096]{0:T(1024)S(1)} %bitcast.210, f32[4096,3]{1,0:T(8,128)S(1)} %copy.104), kind=kCustom, calls=%fused_computation.4.clone.1 | custom fusion | flops 12288 | bytes 163840 | tf_op jit(solution)/shard_map/while/body/scatter-add | solution.py:166
  114.5 10.8 %gather_fusion = f32[4096,3]{1,0:T(8,128)S(1)} fusion(f32[3,256]{0,1:T(8,128)S(1)} %get-tuple-element.550, s32[4096]{0:T(1024)S(1)} %broadcast_clamp_fusion.2), kind=kCustom, calls=%fused_computation.clone.1 | custom fusion | bytes 114688 | tf_op jit(solution)/shard_map/while/body/gather | solution.py:155
  127.4 25.7 %gather_fusion.1 = f32[4096]{0:T(1024)S(1)} fusion(f32[256]{0:T(256)S(1)} %get-tuple-element.553, s32[4096]{0:T(1024)S(1)} %broadcast_clamp_fusion.2), kind=kCustom, calls=%fused_computation.1.clone.1 | custom fusion | bytes 49152 | tf_op jit(solution)/shard_map/while/body/gather | solution.py:156
  153.2 0.9 add_tanh_fusion.3
  154.1 2.0 maximum_add_fusion.4
  156.1 1.2 maximum_add_fusion.5
  159.9 0.9 convolution_convert_fusion.8
  160.8 2.1 copy.99
  162.9 1.4 fusion.226
  164.9 1.7 fusion.227
  167.3 1.2 slice.176
  168.5 1.2 compare_convert_fusion.3
  169.7 1.9 fusion.228
  171.7 2.1 convolution_convert_fusion.9
  173.7 1.9 copy.100
  175.6 2.1 copy.101
  177.7 1.1 fusion.229
  178.7 1.1 fusion.230
  180.3 0.9 multiply_reduce_fusion.6
  182.3 1.2 copy.103
  183.6 1.3 fusion.233
  185.0 1.2 fusion.234
  187.1 25.1 %scatter_fusion = f32[3,256]{0,1:T(8,128)S(1)} fusion(f32[3,256]{0,1:T(8,128)S(1)} %get-tuple-element.518, s32[4096]{0:T(1024)S(1)} %bitcast.210, f32[4096,3]{1,0:T(8,128)S(1)} %copy.104), kind=kCustom, calls=%fused_computation.4.clone.1 | custom fusion | flops 12288 | bytes 163840 | tf_op jit(solution)/shard_map/while/body/scatter-add | solution.py:166
  212.3 5.7 %collective-permute-start.2 = (f32[3,64]{0,1:T(8,128)S(1)}, f32[3,64]{0,1:T(8,128)S(1)}, u32[]{:S(2)}, u32[]{:S(2)}) collective-permute-start(f32[3,64]{0,1:T(8,128)S(1)} %get-tuple-element.295), channel_id=1, source_target_pairs={{0,1},{1,2},{2,3},{3,4},{4,5},{5,6},{6,7},{7,0},{8,9},{9,10},{10,1... | collective-permute-start | bytes 2312 | tf_op jit(solution)/shard_map/ppermute | solution.py:24
  218.0 189.7 %collective-permute-start.3 = (f32[3,64]{0,1:T(8,128)S(1)}, f32[3,64]{0,1:T(8,128)S(1)}, u32[]{:S(2)}, u32[]{:S(2)}) collective-permute-start(f32[3,64]{0,1:T(8,128)S(1)} %get-tuple-element.294), channel_id=1, source_target_pairs={{1,0},{2,1},{3,2},{4,3},{5,4},{6,5},{7,6},{0,7},{9,8},{10,9},{11,1... | collective-permute-start | bytes 2312 | tf_op jit(solution)/shard_map/ppermute | solution.py:26
  408.4 0.8 copy.64
  409.3 1.1 scatter_custom_fusion.1
  410.4 1.1 scatter_custom_fusion.2
  412.3 1.0 broadcast_multiply_fusion.1
  413.3 0.8 maximum_bitcast_fusion.1
  414.1 18.7 %all-to-all-start.1 = ((f32[64,1,2,3,128]{4,2,3,1,0:T(2,128)}), f32[64,1,2,3,128]{4,2,3,1,0:T(2,128)S(1)}, u32[]{:S(2)}, u32[]{:S(2)}) async-start(f32[64,1,2,3,128]{4,2,3,1,0:T(2,128)} %maximum_bitcast_fusion.1), calls=%async_computation.1 | async-start | bytes 393216 | tf_op jit(solution)/shard_map/all_to_all | solution.py:41
  432.9 0.9 maximum_bitcast_fusion
  433.8 16.6 %all-to-all-done.1 = f32[64,1,2,3,128]{4,2,3,1,0:T(2,128)S(1)} async-done(((f32[64,1,2,3,128]{4,2,3,1,0:T(2,128)}), f32[64,1,2,3,128]{4,2,3,1,0:T(2,128)S(1)}, u32[]{:S(2)}, u32[]{:S(2)}) %all-to-all-start.1) | async-done | bytes 196640 | tf_op jit(solution)/shard_map/all_to_all | solution.py:41
  450.4 4.6 all-to-all-start
  455.7 16.8 %all-to-all-done = f32[64,1,2,3,128]{4,2,3,1,0:T(2,128)S(1)} async-done(((f32[64,1,2,3,128]{4,2,3,1,0:T(2,128)}), f32[64,1,2,3,128]{4,2,3,1,0:T(2,128)S(1)}, u32[]{:S(2)}, u32[]{:S(2)}) %all-to-all-start) | async-done | bytes 196640 | tf_op jit(solution)/shard_map/all_to_all | solution.py:41
  (181 shorter events, 28.3 us)
Async XLA Ops:
  0.6 14.8 %copy-start = (bf16[1600,240]{0,1:T(8,128)(2,1)S(1)}, bf16[1600,240]{0,1:T(8,128)(2,1)}, u32[]{:S(2)}) copy-start(bf16[1600,240]{0,1:T(8,128)(2,1)} %param.33) | copy-start | bytes 2304004
  4.9 9.8 %collective-permute-start.1 = (f32[4,64]{1,0:T(4,128)S(1)}, f32[4,64]{1,0:T(4,128)S(1)}, u32[]{:S(2)}, u32[]{:S(2)}) collective-permute-start(f32[4,64]{1,0:T(4,128)S(1)} %get-tuple-element.305), channel_id=1, source_target_pairs={{1,0},{2,1},{3,2},{4,3},{5,4},{6,5},{7,6},{0,7},{9,8},{10,9},{11,1... | collective-permute-start | bytes 3080 | tf_op jit(solution)/shard_map/ppermute | solution.py:26
  5.1 9.6 %collective-permute-start = (f32[4,64]{1,0:T(4,128)S(1)}, f32[4,64]{1,0:T(4,128)S(1)}, u32[]{:S(2)}, u32[]{:S(2)}) collective-permute-start(f32[4,64]{1,0:T(4,128)S(1)} %get-tuple-element.304), channel_id=1, source_target_pairs={{0,1},{1,2},{2,3},{3,4},{4,5},{5,6},{6,7},{7,0},{8,9},{9,10},{10,1... | collective-permute-start | bytes 3080 | tf_op jit(solution)/shard_map/ppermute | solution.py:24
  14.7 0.6 copy-start.24
  15.4 40.0 %copy-start.1 = (f32[3,256]{0,1:T(8,128)}, f32[3,256]{0,1:T(8,128)S(1)}, u32[]{:S(2)}) copy-start(f32[3,256]{0,1:T(8,128)S(1)} %get-tuple-element.550) | copy-start | bytes 9220 | tf_op jit(solution)/shard_map/while
  16.2 39.3 %copy-start.18 = (pred[32,128]{1,0:T(8,128)(4,1)}, pred[32,128]{1,0:T(8,128)(4,1)S(1)}, u32[]{:S(2)}) copy-start(pred[32,128]{1,0:T(8,128)(4,1)S(1)} %get-tuple-element.474) | copy-start | bytes 12292 | tf_op jit(solution)/shard_map/while
  16.2 0.6 copy-start.10
  28.4 27.1 %copy-start.12 = (f32[32,128]{1,0:T(8,128)}, f32[32,128]{1,0:T(8,128)S(1)}, u32[]{:S(2)}) copy-start(f32[32,128]{1,0:T(8,128)S(1)} %multiply_reduce_fusion.5) | copy-start | bytes 49156 | tf_op jit(solution)/shard_map/while
  29.7 26.7 %copy-start.20 = (f32[25]{0:T(128)}, f32[25]{0:T(128)S(1)}, u32[]{:S(2)}) copy-start(f32[25]{0:T(128)S(1)} %get-tuple-element.476) | copy-start | bytes 304 | tf_op jit(solution)/shard_map/while
  29.7 26.7 %copy-start.22 = (f32[25]{0:T(128)}, f32[25]{0:T(128)S(1)}, u32[]{:S(2)}) copy-start(f32[25]{0:T(128)S(1)} %get-tuple-element.477) | copy-start | bytes 304 | tf_op jit(solution)/shard_map/while
  55.5 2.9 copy-start.14
  59.6 0.7 copy-start.8
  60.5 0.6 copy-start.16
  61.6 0.6 copy-start.7
  66.7 0.6 copy-start.6
  80.0 3.5 copy-start.17
  82.6 1.9 copy-start.4
  85.9 1.4 copy-start.3
  85.9 1.4 copy-start.15
  85.9 1.4 copy-start.21
  85.9 1.4 copy-start.23
  87.2 1.3 slice-start
  87.2 1.3 copy-start.13
  87.2 1.3 copy-start.19
  87.2 1.3 copy-start.5
  87.3 1.3 copy-start.9
  88.5 0.9 copy-start.11
  88.8 24.3 %copy-start.2 = (f32[3,256]{0,1:T(8,128)S(1)}, f32[3,256]{0,1:T(8,128)}, u32[]{:S(2)}) copy-start(f32[3,256]{0,1:T(8,128)} %copy-done.1) | copy-start | bytes 9220 | tf_op jit(solution)/shard_map/while
  113.1 40.0 %copy-start.1 = (f32[3,256]{0,1:T(8,128)}, f32[3,256]{0,1:T(8,128)S(1)}, u32[]{:S(2)}) copy-start(f32[3,256]{0,1:T(8,128)S(1)} %get-tuple-element.550) | copy-start | bytes 9220 | tf_op jit(solution)/shard_map/while
  113.9 39.3 %copy-start.18 = (pred[32,128]{1,0:T(8,128)(4,1)}, pred[32,128]{1,0:T(8,128)(4,1)S(1)}, u32[]{:S(2)}) copy-start(pred[32,128]{1,0:T(8,128)(4,1)S(1)} %get-tuple-element.474) | copy-start | bytes 12292 | tf_op jit(solution)/shard_map/while
  113.9 0.6 copy-start.10
  126.1 27.1 %copy-start.12 = (f32[32,128]{1,0:T(8,128)}, f32[32,128]{1,0:T(8,128)S(1)}, u32[]{:S(2)}) copy-start(f32[32,128]{1,0:T(8,128)S(1)} %multiply_reduce_fusion.5) | copy-start | bytes 49156 | tf_op jit(solution)/shard_map/while
  127.4 26.7 %copy-start.20 = (f32[25]{0:T(128)}, f32[25]{0:T(128)S(1)}, u32[]{:S(2)}) copy-start(f32[25]{0:T(128)S(1)} %get-tuple-element.476) | copy-start | bytes 304 | tf_op jit(solution)/shard_map/while
  127.4 26.7 %copy-start.22 = (f32[25]{0:T(128)}, f32[25]{0:T(128)S(1)}, u32[]{:S(2)}) copy-start(f32[25]{0:T(128)S(1)} %get-tuple-element.477) | copy-start | bytes 304 | tf_op jit(solution)/shard_map/while
  153.2 2.9 copy-start.14
  157.3 0.7 copy-start.8
  158.1 0.6 copy-start.16
  159.3 0.6 copy-start.7
  164.3 0.6 copy-start.6
  177.7 3.5 copy-start.17
  180.3 1.9 copy-start.4
  183.6 1.4 copy-start.3
  183.6 1.4 copy-start.15
  183.6 1.4 copy-start.21
  183.6 1.4 copy-start.23
  184.9 1.3 slice-start
  184.9 1.3 copy-start.13
  184.9 1.3 copy-start.19
  184.9 1.3 copy-start.5
  184.9 1.3 copy-start.9
  186.2 0.9 copy-start.11
  186.5 25.8 %copy-start.2 = (f32[3,256]{0,1:T(8,128)S(1)}, f32[3,256]{0,1:T(8,128)}, u32[]{:S(2)}) copy-start(f32[3,256]{0,1:T(8,128)} %copy-done.1) | copy-start | bytes 9220 | tf_op jit(solution)/shard_map/while
  212.3 197.0 %collective-permute-start.2 = (f32[3,64]{0,1:T(8,128)S(1)}, f32[3,64]{0,1:T(8,128)S(1)}, u32[]{:S(2)}, u32[]{:S(2)}) collective-permute-start(f32[3,64]{0,1:T(8,128)S(1)} %get-tuple-element.295), channel_id=1, source_target_pairs={{0,1},{1,2},{2,3},{3,4},{4,5},{5,6},{6,7},{7,0},{8,9},{9,10},{10,1... | collective-permute-start | bytes 2312 | tf_op jit(solution)/shard_map/ppermute | solution.py:24
  218.0 192.4 %collective-permute-start.3 = (f32[3,64]{0,1:T(8,128)S(1)}, f32[3,64]{0,1:T(8,128)S(1)}, u32[]{:S(2)}, u32[]{:S(2)}) collective-permute-start(f32[3,64]{0,1:T(8,128)S(1)} %get-tuple-element.294), channel_id=1, source_target_pairs={{1,0},{2,1},{3,2},{4,3},{5,4},{6,5},{7,6},{0,7},{9,8},{10,9},{11,1... | collective-permute-start | bytes 2312 | tf_op jit(solution)/shard_map/ppermute | solution.py:26
  414.1 36.2 %all-to-all-start.1 = ((f32[64,1,2,3,128]{4,2,3,1,0:T(2,128)}), f32[64,1,2,3,128]{4,2,3,1,0:T(2,128)S(1)}, u32[]{:S(2)}, u32[]{:S(2)}) async-start(f32[64,1,2,3,128]{4,2,3,1,0:T(2,128)} %maximum_bitcast_fusion.1), calls=%async_computation.1 | async-start | bytes 393216 | tf_op jit(solution)/shard_map/all_to_all | solution.py:41
  450.4 22.2 %all-to-all-start = ((f32[64,1,2,3,128]{4,2,3,1,0:T(2,128)}), f32[64,1,2,3,128]{4,2,3,1,0:T(2,128)S(1)}, u32[]{:S(2)}, u32[]{:S(2)}) async-start(f32[64,1,2,3,128]{4,2,3,1,0:T(2,128)} %maximum_bitcast_fusion), calls=%async_computation | async-start | bytes 393216 | tf_op jit(solution)/shard_map/all_to_all | solution.py:41
where the time goes:
time: 482 us; the launch traced here: 473 us
  starting transfers between devices  219 us (45%)
  local copies, waits for them, and re-layouts  109 us (23%)
  other arithmetic  72.6 us (15%)
  matrix products  36.8 us (8%)
  waiting for transfers between devices  33.6 us (7%)
    ppermute x2, starting transfers between devices, padded_2(): lax.ppermute(head, axis, [((i + 1) % count, i) for i in range(count)])  190 us
    gather x2, local copies, waits for them, and re-layouts, block_gradient(): around_hydrogen = wide_hydrogen[flat_rows].reshape(BLOCK, -1)  51.5 us
    scatter-add x2, other arithmetic, block_gradient(): gradient = gradient.at[:, flat_rows].add(grad_around.reshape(3, -1))  48.7 us
    all_to_all x2, waiting for transfers between devices, sum_at_owner(): lax.all_to_all(pieces, axis, split_axis=0, concat_axis=0, tiled=True)  33.5 us
    all_to_all x2, starting transfers between devices, sum_at_owner(): lax.all_to_all(pieces, axis, split_axis=0, concat_axis=0, tiled=True)  23.4 us
    gather x4, local copies, waits for them, and re-layouts, block_gradient(): beside_all = extended[:, flat_rows].reshape(3, BLOCK, -1)  22.8 us
  transfers between devices with their start and end apart: 6, of which 3 were waited for; matrix products, arithmetic and copies ran while one was open for 3% of the time, Pallas kernels for 0%

commit v1 on v0

v1 whole, which is shorter than its diff:
```python
import functools

import jax
import jax.numpy as jnp
import numpy as np
from jax import lax
from jax.experimental import pallas as pl
from jax.experimental.pallas import tpu as pltpu
from jax.sharding import PartitionSpec as P

BEADS = 64
N_SLAB = 8
SHARE = 16
LANES = 128
STEP = 0.25
HEAVY = 16.0
BLK = 8
CHUNK = 64
F32 = jnp.float32
BF16 = jnp.bfloat16
NT = (((1,), (1,)), ((), ()))
HIGH = lax.Precision.HIGHEST


def two_feature(row):
    if row < 24:
        return row
    if row < 48:
        return row + 1
    if row < 52:
        return (24, 49)[(row - 48) % 2]
    return -1


def three_feature(row):
    if row < 48:
        return two_feature(row)
    if row < 96:
        return 50 + two_feature(row - 48)
    if row < 100:
        return (24, 49, 74, 99)[row - 96]
    return -1


def selections():
    one_of = [k if k < 24 else 24 if k < 28 else -1 for k in range(32)]
    s1 = np.zeros((32, 25), np.float32)
    for k, f in enumerate(one_of):
        if f >= 0:
            s1[k, f] = 1
    a2 = np.zeros((56, 50), np.float32)
    for k in range(56):
        if two_feature(k) >= 0:
            a2[k, two_feature(k)] = 1
    b1 = np.zeros((25, 32), np.float32)
    for f in range(25):
        b1[f, f] = 1
    a3 = np.zeros((104, 100), np.float32)
    where = np.zeros((104,), np.int32)
    where[100:] = 127
    for k in range(104):
        if three_feature(k) >= 0:
            a3[k, three_feature(k)] = 1
            where[three_feature(k)] = k
    b2 = np.zeros((50, 56), np.float32)
    for k in range(50):
        b2[two_feature(k), k] = 1
    spread = np.full((16, LANES), 127, np.int32)
    fold = np.zeros((13 * LANES, LANES), np.float32)
    for g in range(13):
        for lane in range(LANES):
            e = 8 * g + lane // 16
            spread[g, lane] = where[e]
            if e < 100:
                fold[g * LANES + lane, where[e]] = 1
    return s1, a2, b1, a3, b2, spread, fold


def mode_matrices():
    n = BEADS
    j, k = np.arange(n)[:, None], np.arange(n)[None, :]
    angle = 2 * np.pi * ((j * k) % n) / n
    basis = np.where(
        k == 0,
        1 / np.sqrt(n),
        np.where(
            k < n // 2,
            np.sqrt(2 / n) * np.cos(angle),
            np.where(k == n // 2, np.where(j % 2 == 0, 1.0, -1.0) / np.sqrt(n), np.sqrt(2 / n) * np.sin(angle)),
        ),
    )
    sine = np.sin(np.pi * np.arange(n) / n)
    ratio = 2 * sine
    theta = 1.2 * n * sine
    travel = np.where(np.arange(n) == 0, 1.0, np.sin(theta) / np.where(np.arange(n) == 0, 1.0, ratio))
    return tuple(
        ((basis * d[None, :]) @ basis.T).astype(np.float32)
        for d in (np.cos(theta), travel, ratio * np.sin(theta))
    )


def lanes_of(table, index):
    return jnp.take_along_axis(table, index, axis=1, mode="promise_in_bounds")


def spread_rows(row, count):
    return jnp.broadcast_to(row, (count, row.shape[1]))


def own_tile(pos, types, halo):
    hydrogen = jnp.where(types == 1, 1.0, 0.0).astype(F32)
    mine = jnp.concatenate([pos, hydrogen], axis=0)
    wide = jnp.concatenate([mine, mine], axis=0)
    sent = lanes_of(wide, spread_rows(halo, 8))
    return jnp.where(lax.broadcasted_iota(jnp.int32, (8, LANES), 0) < 4, wide, sent)


def thirds(row):
    high = row.astype(BF16).astype(F32)
    rest = row - high
    mid = rest.astype(BF16).astype(F32)
    return high, mid, rest - mid


def bias_rows(bias, first, count):
    high, mid, low = thirds(bias)
    at = lax.broadcasted_iota(jnp.int32, (count, bias.shape[1]), 0)
    return jnp.where(at == first, high, jnp.where(at == first + 1, mid, jnp.where(at == first + 2, low, 0.0)))


def prepare_weights(scale, shift, w2, b2, w3, b3, s1, a2, p1, a3, p2, w2t, w3t, cols):
    dot = functools.partial(lax.dot_general, preferred_element_type=F32)
    two = dot(a2[...], w2[...], NT).astype(BF16)
    two = dot(two, p1[...], (((1,), (0,)), ((), ())))
    two = two + dot(a2[...], bias_rows(b2[...], 28, 32).astype(BF16), NT)
    w2t[...] = two.astype(BF16)
    three = dot(a3[...], w3[...], NT).astype(BF16)
    three = dot(three, p2[...], (((1,), (0,)), ((), ())))
    three = three + dot(a3[...], bias_rows(b3[...], 52, 56).astype(BF16), NT)
    w3t[...] = three.astype(BF16)
    at = lax.broadcasted_iota(jnp.int32, (32, LANES), 0)
    ones = jnp.where((at >= 28) & (at < 31), 20.0, 0.0)
    for kind in range(2):
        for n, ref in enumerate((scale, shift)):
            col = dot(s1[...], spread_rows(ref[kind : kind + 1, :], LANES), NT, precision=HIGH)
            cols[2 * n + kind] = col + ones if n else col


def force_kernel(
    tile, nb, w2t, w3t, cols, spread, fold_hbm, fit1_hbm, fit2_hbm, fit3_hbm, c1, c2, c3, readout,
    out,
    env, geo, order, count, hc, three, feats, gfeats, qs, ps, scat, fold, fit1, fit2, fit3, sems,
):
    me = lax.axis_index("slab")
    loads = [
        pltpu.make_async_copy(src, dst, sems.at[n])
        for n, (src, dst) in enumerate(
            ((fit1_hbm, fit1), (fit2_hbm, fit2), (fit3_hbm, fit3), (fold_hbm, fold))
        )
    ]
    for load in loads:
        load.start()
    dot = functools.partial(lax.dot_general, preferred_element_type=F32)
    NN = (((1,), (0,)), ((), ()))
    lane8 = lax.broadcasted_iota(jnp.int32, (8, LANES), 1)
    row8 = lax.broadcasted_iota(jnp.int32, (8, LANES), 0)

    for s in range(N_SLAB):
        count[s] = jnp.sum(jnp.where(nb[s][:, 0:1] >= 0, 1.0, 0.0)).astype(jnp.int32)
    total = jnp.int32(0)
    for s in range(N_SLAB):
        for j in range(SHARE):
            order[total + j] = s * SHARE + j
        total = total + count[s]
    for j in range(BLK):
        order[total + j] = N_SLAB * SHARE
    env[pl.ds(N_SLAB * SHARE * 8, 8), :] = jnp.zeros((8, LANES), F32)

    def own_row(s, half):
        return (row8 + half * 8) * 8 + lax.rem(me - s + N_SLAB, N_SLAB)

    def geometry(s, half):
        before = lax.rem(s + N_SLAB - 1, N_SLAB)
        after = lax.rem(s + 1, N_SLAB)
        idx = nb[s, half * 8 : half * 8 + 8, :]
        low = idx & 127
        far = idx >= 128
        own = tile[s]
        edge = pltpu.roll(jnp.where(lane8 >= 64, tile[before], tile[after]), 64, 1)
        centre_at = own_row(s, half)
        base = s * SHARE + half * 8
        got = []
        for c in range(4):
            near = lanes_of(spread_rows(own[c : c + 1], 8), low)
            there = lanes_of(spread_rows(edge[4 + c : 5 + c], 8), low)
            got.append(jnp.where(far, there, near))
        mid = [lanes_of(spread_rows(own[c : c + 1], 8), centre_at) for c in range(4)]
        off = [got[c] - mid[c] for c in range(3)]
        d2 = off[0] * off[0] + off[1] * off[1] + off[2] * off[2]
        inv = lax.rsqrt(d2 + 0.25)
        fsw = jnp.where(idx >= 0, jnp.maximum(1.0 - d2 * (1.0 / 16.0), 0.0), 0.0)
        strength = fsw * fsw * inv
        si = strength * inv
        at = pl.ds(base, 8)
        for n, value in enumerate((*off, inv, fsw)):
            geo[n, at, :] = value
        for n, value in enumerate((strength, si * off[0], si * off[1], si * off[2], got[3], mid[3])):
            env[pl.ds(base * 8 + n, 8, stride=8), :] = value

    for s in range(N_SLAB):
        geometry(s, 0)

    def second_half(fn):
        def step(s, carry):
            @pl.when(count[s] > 8)
            def _():
                fn(s, 1)
            return carry

        lax.fori_loop(0, N_SLAB, step, 0)

    second_half(geometry)

    sc0, sc1, sh0, sh1 = 0, 1, 2, 3

    def forward(block, carry):
        first = block * BLK
        e, one, done = [], [], []
        for b in range(BLK):
            row = order[first + b]
            v = env[pl.ds(pl.multiple_of(row * 8, 8), 8), :]
            e.append(v)
            hyd = v[4:5] > 0.5
            sc = jnp.where(hyd, cols[sc1], cols[sc0])
            t = jnp.tanh(v[0:1] * sc + jnp.where(hyd, cols[sh1], cols[sh0]))
            one.append((t, (1.0 - t * t) * sc))
            hc[pl.ds(first + b, 1), :] = v[5:6]
        x = jnp.concatenate([a.astype(BF16) for pair in one for a in pair], axis=1)
        z = dot(w2t[...], x, NN)
        two = []
        for b in range(BLK):
            t1, d1 = one[b]
            t = jnp.tanh(z[:, 256 * b : 256 * b + 128])
            d = (1.0 - t * t) * z[:, 256 * b + 128 : 256 * b + 256]
            two.append((
                t + jnp.concatenate([t1[:24], t1[:24], t1[24:]], axis=0),
                d + jnp.concatenate([d1[:24], d1[:24], d1[24:]], axis=0),
            ))
        x = jnp.concatenate([a.astype(BF16) for pair in two for a in pair], axis=1)
        z = dot(w3t[...], x, NN)
        for b in range(BLK):
            t2, d2 = two[b]
            t = jnp.tanh(z[:, 256 * b : 256 * b + 128])
            d = (1.0 - t * t) * z[:, 256 * b + 128 : 256 * b + 256]
            l3 = (t + jnp.concatenate([t2[:48], t2[:48], t2[48:]], axis=0)).astype(BF16)
            d3 = (d + jnp.concatenate([d2[:48], d2[:48], d2[48:]], axis=0)).astype(BF16)
            three[first + b] = jnp.concatenate([l3, d3], axis=1)
            f = dot(e[b].astype(BF16), l3, NT) * (1.0 / 128.0)
            feats[pl.ds(pl.multiple_of((first + b) * 8, 8), 8), :] = jnp.concatenate(
                [f, jnp.zeros((8, 24), F32)], axis=1
            )
        return carry

    blocks = lax.div(total + (BLK - 1), BLK)
    lax.fori_loop(0, blocks, forward, 0)

    for load in loads:
        load.wait()

    lane_m = lax.broadcasted_iota(jnp.int32, (CHUNK, LANES), 1)

    def fit(chunk, carry):
        base = chunk * (CHUNK * 8)
        fs = [feats[pl.ds(base + c, CHUNK, stride=8), :] for c in range(4)]
        tiled = [lanes_of(f, lane_m & 15) for f in fs]
        spreads = [
            [lanes_of(f, spread_rows(spread[g : g + 1, :], CHUNK)) for f in fs] for g in range(13)
        ]
        desc = [sum(spreads[g][c] * tiled[c] for c in range(4)) for g in range(13)]
        desc = jnp.concatenate(desc, axis=1).astype(BF16)[:, :1600]
        f1 = jnp.tanh(dot(desc, fit1[...], NN) + c1[...])
        t2 = jnp.tanh(dot(f1.astype(BF16), fit2[...], NN) + c2[...])
        f2 = t2 + f1
        t3 = jnp.tanh(dot(f2.astype(BF16), fit3[...], NN) + c3[...])
        h = hc[pl.ds(chunk * CHUNK, CHUNK), :]
        h = jnp.concatenate([h, h], axis=1)[:, :240]
        g3 = readout[0:1, :] + h * (readout[1:2, :] - readout[0:1, :])
        g2 = g3 + dot((g3 * (1.0 - t3 * t3)).astype(BF16), fit3[...], NT)
        g1 = g2 + dot((g2 * (1.0 - t2 * t2)).astype(BF16), fit2[...], NT)
        gd = dot((g1 * (1.0 - f1 * f1)).astype(BF16), fit1[...], NT)
        gd = jnp.concatenate([gd, jnp.zeros((CHUNK, 64), F32)], axis=1)
        parts = [gd[:, g * LANES : (g + 1) * LANES] for g in range(13)]
        for c in range(4):
            left = jnp.concatenate([p * tiled[c] for p in parts], axis=1).astype(BF16)
            left = dot(left, fold[...], NN)
            right = sum(parts[g] * spreads[g][c] for g in range(13))
            for shift in (64, 32, 16):
                right = right + pltpu.roll(right, shift, 1)
            gf = left + jnp.where(lane_m < 16, right, 0.0)
            gfeats[pl.ds(base + c, CHUNK, stride=8), :] = gf * (1.0 / 128.0)
        return carry

    lax.fori_loop(0, lax.div(total + (CHUNK - 1), CHUNK), fit, 0)

    def back(block, carry):
        first = block * BLK
        for b in range(BLK):
            row = order[first + b]
            gf = gfeats[pl.ds(pl.multiple_of((first + b) * 8, 8), 8), :][:, :104]
            qp = dot(gf.astype(BF16), three[first + b], NN)
            at = pl.ds(pl.multiple_of(row * 8, 8), 8)
            qs[at, :] = qp[:, :128]
            ps[at, :] = qp[:, 128:]
        return carry

    lax.fori_loop(0, blocks, back, 0)

    sub = lax.broadcasted_iota(jnp.int32, (LANES, LANES), 0)

    def scatter(s, half):
        base = s * SHARE + half * 8
        at = pl.ds(base, 8)
        idx = nb[s, half * 8 : half * 8 + 8, :]
        off = [geo[n, at, :] for n in range(3)]
        inv, fsw = geo[3, at, :], geo[4, at, :]
        q = [qs[pl.ds(base * 8 + n, 8, stride=8), :] for n in range(4)]
        p = [ps[pl.ds(base * 8 + n, 8, stride=8), :] for n in range(4)]
        inv3 = 0.5 * inv * inv * inv
        strength = fsw * fsw * inv
        qo = q[1] * off[0] + q[2] * off[1] + q[3] * off[2]
        po = p[1] * off[0] + p[2] * off[1] + p[3] * off[2]
        gs = q[0] + inv * qo + strength * (p[0] + inv * po)
        gd2 = -gs * (fsw * inv * 0.125 + fsw * fsw * inv3) - qo * strength * inv3
        si = strength * inv
        g = [jnp.where(idx >= 0, q[1 + c] * si + 2.0 * off[c] * gd2, 0.0) for c in range(3)]
        near = idx < 128
        centre_at = own_row(s, half) == lane8
        grad = jnp.zeros((8, LANES), F32)
        for c in range(3):
            scat[pl.ds(base * 8 + c, 8, stride=8), :] = jnp.where(near, g[c], 0.0)
            scat[pl.ds(base * 8 + 3 + c, 8, stride=8), :] = jnp.where(near, 0.0, g[c])
            total_c = jnp.sum(g[c], axis=1, keepdims=True)
            line = jnp.sum(jnp.where(centre_at, -total_c, 0.0), axis=0, keepdims=True)
            grad = jnp.where(row8 == c, line, grad)
        lhs, rhs = [], []
        for j in range(8):
            lhs.append(scat[pl.ds((base + j) * 8, 8), :].astype(BF16))
            low = nb[s, half * 8 + j : half * 8 + j + 1, :] & 127
            rhs.append(jnp.where(sub == low, 1.0, 0.0).astype(BF16))
        grad = grad + dot(jnp.concatenate(lhs, axis=1), jnp.concatenate(rhs, axis=1), NT)
        if half == 0:
            feats[pl.ds(s * 8, 8), :] = grad
        else:
            feats[pl.ds(s * 8, 8), :] += grad

    for s in range(N_SLAB):
        scatter(s, 0)
    second_half(scatter)
    grads = [feats[pl.ds(s * 8, 8), :] for s in range(N_SLAB)]
    for s in range(N_SLAB):
        edge = jnp.where(lane8 < 64, grads[(s + 1) % N_SLAB], grads[(s - 1) % N_SLAB])
        out[s] = jnp.where(row8 < 3, grads[s], edge)


def force_call(tile, nb, w2t, w3t, cols, fit):
    fit1, b1, fit2, b2, fit3, b3, readout = fit
    _, _, _, _, _, spread, fold = selections()
    rows = N_SLAB * SHARE
    vm = pl.BlockSpec(memory_space=pltpu.VMEM)
    anyw = pl.BlockSpec(memory_space=pl.ANY)
    return pl.pallas_call(
        force_kernel,
        out_shape=jax.ShapeDtypeStruct((N_SLAB, 8, LANES), F32),
        in_specs=[vm] * 6 + [anyw] * 4 + [vm] * 4,
        out_specs=vm,
        scratch_shapes=[
            pltpu.VMEM(((rows + 1) * 8, LANES), F32),
            pltpu.VMEM((5, rows, LANES), F32),
            pltpu.SMEM((rows + 24,), jnp.int32),
            pltpu.SMEM((N_SLAB,), jnp.int32),
            pltpu.VMEM((rows + 8, LANES), F32),
            pltpu.VMEM((rows + 8, 104, 256), BF16),
            pltpu.VMEM(((rows + 8) * 8, LANES), F32),
            pltpu.VMEM(((rows + 8) * 8, LANES), F32),
            pltpu.VMEM(((rows + 1) * 8, LANES), F32),
            pltpu.VMEM(((rows + 1) * 8, LANES), F32),
            pltpu.VMEM((rows * 8, LANES), F32),
            pltpu.VMEM((13 * LANES, LANES), BF16),
            pltpu.VMEM((1600, 240), BF16),
            pltpu.VMEM((240, 240), BF16),
            pltpu.VMEM((240, 240), BF16),
            pltpu.SemaphoreType.DMA((4,)),
        ],
        compiler_params=pltpu.CompilerParams(vmem_limit_bytes=48 << 20),
        name="force",
    )(
        tile, nb, w2t, w3t, cols, jnp.asarray(spread), jnp.asarray(fold, BF16),
        fit1, fit2, fit3, b1[None], b2[None], b3[None], readout,
    )


def prepare_kernel(pos, types, halo, scale, shift, w2, b2, w3, b3, s1, a2, p1, a3, p2, tile, w2t, w3t, cols):
    tile[...] = own_tile(pos[...], types[...], halo[...])
    prepare_weights(scale, shift, w2, b2, w3, b3, s1, a2, p1, a3, p2, w2t, w3t, cols)


def kick_kernel(msgs, vel, types, halo, forces, kicked):
    got = msgs[0]
    for s in range(1, N_SLAB):
        got = got + msgs[s]
    bins = pltpu.roll(spread_rows(halo[...], 8), 64, 1)[0:1]
    hit = jnp.where(lax.broadcasted_iota(jnp.int32, (LANES, LANES), 0) == bins, 1.0, 0.0)
    back = lax.dot_general(got, hit, NT, preferred_element_type=F32, precision=HIGH)
    force = -(got[0:3] + back[3:6])
    forces[...] = force
    kicked[...] = vel[...] + STEP * jnp.where(types[...] == 1, 1.0, 1.0 / HEAVY) * force


def local(
    positions, velocities, atom_types, live_atoms, halo_rows, neighbours,
    type_scale, type_shift, embed_two, embed_bias_two, embed_three, embed_bias_three,
    fit_first, fit_bias_first, fit_second, fit_bias_second, fit_third, fit_bias_third, fit_readout,
):
    del live_atoms
    pos, vel, types = positions[:, 0, :], velocities[:, 0, :], atom_types[None]
    s1, a2, p1, a3, p2, _, _ = selections()
    tile, w2t, w3t, cols = pl.pallas_call(
        prepare_kernel,
        out_shape=(
            jax.ShapeDtypeStruct((8, LANES), F32),
            jax.ShapeDtypeStruct((56, 32), BF16),
            jax.ShapeDtypeStruct((104, 56), BF16),
            jax.ShapeDtypeStruct((4, 32, LANES), F32),
        ),
        name="prepare",
    )(
        pos, types, halo_rows, type_scale, type_shift, embed_two, embed_bias_two[None],
        embed_three, embed_bias_three[None], jnp.asarray(s1), jnp.asarray(a2, BF16),
        jnp.asarray(p1, BF16), jnp.asarray(a3, BF16), jnp.asarray(p2, BF16),
    )
    me = lax.axis_index("slab")
    dealt = jnp.moveaxis(neighbours.reshape(SHARE, N_SLAB, LANES), 1, 0).astype(F32)
    dealt = jnp.roll(dealt, me, axis=0)
    parcel = jnp.concatenate([jnp.broadcast_to(tile, (N_SLAB, 8, LANES)), dealt], axis=1)
    parcel = lax.all_to_all(parcel, "slab", 0, 0, tiled=True)
    nb = parcel[:, 8:].astype(jnp.int32)
    msgs = force_call(
        parcel[:, :8], nb, w2t, w3t, cols,
        (fit_first, fit_bias_first, fit_second, fit_bias_second, fit_third, fit_bias_third, fit_readout),
    )
    msgs = lax.all_to_all(msgs, "slab", 0, 0, tiled=True)
    forces, kicked = pl.pallas_call(
        kick_kernel,
        out_shape=(jax.ShapeDtypeStruct((3, LANES), F32),) * 2,
        name="kick",
    )(msgs, vel, types, halo_rows)
    own = lax.axis_index("bead")
    cos, travel, spring = (jnp.asarray(m) for m in mode_matrices())
    col = lambda m: lax.dynamic_index_in_dim(m, own, 1, keepdims=False)[:BEADS_HERE, None, None]
    mixed = jnp.stack(
        [
            col(cos) * pos + col(travel) * kicked,
            col(-spring) * pos + col(cos) * kicked,
        ],
        axis=1,
    )
    mixed = lax.all_to_all(mixed, "bead", 0, 0, tiled=True).sum(axis=0)
    return mixed[0][:, None, :], mixed[1][:, None, :], forces[:, None, :]


BEADS_HERE = BEADS


def solution(mesh):
    wide = P(None, "bead", "slab")
    return jax.shard_map(
        local,
        mesh=mesh,
        in_specs=(wide, wide, P("slab"), P("slab"), P("slab", None), P("slab", None)) + (P(),) * 13,
        out_specs=(wide, wide, wide),
        check_vma=False,
    )
```

time: 482 us -> 79.9 us (0.17)
  the two profiles are of different devices: /device:TPU:6 before, /device:TPU:2 now
where the time goes in v1:
time: 79.9 us; the launch traced here: 79.3 us
  starting transfers between devices  28.3 us (35%)
  waiting for transfers between devices  24.5 us (31%)
  Pallas kernels  14.4 us (18%)
  local copies, waits for them, and re-layouts  9.44 us (12%)
  other arithmetic  1.79 us (2%)
  between operations  0.85 us (1%)
    all_to_all x1, waiting for transfers between devices, local(): mixed = lax.all_to_all(mixed, 'bead', 0, 0, tiled=True).sum(axis=0)  18.9 us
    all_to_all x1, starting transfers between devices, local(): mixed = lax.all_to_all(mixed, 'bead', 0, 0, tiled=True).sum(axis=0)  14.4 us
    pallas_call x1, Pallas kernels, force_call(): pl.pallas_call(force_kernel, out_shape=jax.ShapeDtypeStruct((N_SLAB, 8, L...  10.5 us
    all_to_all x1, starting transfers between devices, local(): parcel = lax.all_to_all(parcel, 'slab', 0, 0, tiled=True)  9.15 us
    unnamed x38, local copies, waits for them, and re-layouts  5.89 us
    all_to_all x1, starting transfers between devices, local(): msgs = lax.all_to_all(msgs, 'slab', 0, 0, tiled=True)  4.71 us
    all_to_all x1, waiting for transfers between devices, local(): parcel = lax.all_to_all(parcel, 'slab', 0, 0, tiled=True)  2.82 us
    all_to_all x1, waiting for transfers between devices, local(): msgs = lax.all_to_all(msgs, 'slab', 0, 0, tiled=True)  2.72 us
  transfers between devices with their start and end apart: 3, of which 3 were waited for; matrix products, arithmetic and copies ran while one was open for 4% of the time, Pallas kernels for 0%

profile of v1, /device:TPU:2, one launch (start us, length us, event | category | flops | bytes accessed | tf_op | source)
XLA Modules:
  0.0 79.3 jit_solution(2531501240903016935)
XLA Ops:
  0.6 0.0 copy-start.11
  0.7 0.9 %convert_bitcast_fusion = f32[16,8,128]{2,1,0:T(8,128)S(1)} fusion(s32[128,128]{1,0:T(8,128)} %param.33), kind=kLoop, calls=%fused_computation.9 | loop fusion | flops 16384 | bytes 131072 | tf_op jit(solution)/shard_map/convert_element_type | solution.py:442
  1.6 1.3 %copy.50 = f32[3,1,128]{2,0,1:T(4,128)} copy(f32[3,1,128]{2,1,0:T(1,128)} %param.29) | data formatting | bytes 3072
  2.9 2.3 %prepare.1 = (f32[8,128]{1,0:T(8,128)}, bf16[56,32]{1,0:T(8,128)(2,1)}, bf16[104,56]{1,0:T(8,128)(2,1)}, f32[4,32,128]{2,1,0:T(8,128)}) custom-call(f32[3,128]{1,0:T(4,128)} %bitcast.32, s32[1,128]{1,0:T(1,128)} %bitcast.35, s32[1,128]{1,0:T(1,128)} %halo.3, f32[2,25]{1,0:T(2,128)} %scale.1, f32[2,25]{1,0:T(2,128)} %shift.1, bf16[25,50]{1,0:T(8,128)(2,1)} %w2.1, ...), custom_call_target="tpu_custom_call" | custom-call | tf_op jit(solution)/shard_map/prepare/pallas_call | solution.py:427
  5.2 0.7 broadcast_in_dim.33
  5.9 0.6 pad_maximum_fusion.1
  6.5 9.1 %all-to-all-start = ((f32[8,24,128]{2,1,0:T(8,128)}), f32[8,24,128]{2,1,0:T(8,128)S(1)}, u32[]{:S(2)}, u32[]{:S(2)}) async-start(f32[8,24,128]{2,1,0:T(8,128)} %pad_maximum_fusion.1), calls=%async_computation | async-start | bytes 196608 | tf_op jit(solution)/shard_map/all_to_all | solution.py:445
  15.7 0.0 copy-done.11
  15.7 0.0 copy-start
  15.7 0.0 copy-start.2
  15.7 0.0 copy-start.5
  15.7 0.0 copy-start.6
  15.7 0.7 copy.40.fit1_hbm
  16.5 0.0 copy-start.1
  16.5 0.7 fusion.1
  17.2 2.8 %all-to-all-done = f32[8,24,128]{2,1,0:T(8,128)S(1)} async-done(((f32[8,24,128]{2,1,0:T(8,128)}), f32[8,24,128]{2,1,0:T(8,128)S(1)}, u32[]{:S(2)}, u32[]{:S(2)}) %all-to-all-start) | async-done | bytes 98336 | tf_op jit(solution)/shard_map/all_to_all | solution.py:445
  20.0 0.0 copy-start.4
  20.1 0.0 copy-start.3
  20.1 0.0 copy-start.9
  20.1 0.0 copy-start.10
  20.1 0.0 copy-start.7
  20.1 0.0 copy-start.8
  20.1 0.0 copy-done
  20.1 0.0 copy-done.2
  20.1 0.0 copy-done.5
  20.2 0.0 copy-done.6
  20.2 0.0 copy-done.1
  20.2 0.6 copy-done.4
  20.8 0.1 copy-done.3
  20.9 0.0 copy-done.9
  20.9 0.0 copy-done.10
  20.9 0.0 copy-done.7
  20.9 0.0 copy-done.8
  20.9 10.5 %force.1 = f32[8,8,128]{2,1,0:T(8,128)} custom-call(f32[8,8,128]{2,1,0:T(8,128)S(1)} %slice.16.tile, s32[8,16,128]{2,1,0:T(8,128)S(1)} %slice_convert_fusion.nb, bf16[56,32]{1,0:T(8,128)(2,1)S(1)} %copy-done.5, bf16[104,56]{1,0:T(8,128)(2,1)S(1)} %copy-done.4, f32[4,32,128]{2,1,0:T(8,128)S(1)} %copy-done.3, s32[16,128]{1,0:T(8,128)S(1)} %copy-done.6, ...), custom_call_target="tpu_custom_call" | custom-call | tf_op jit(solution)/shard_map/force/pallas_call | solution.py:371
  31.4 4.7 %all-to-all-start.1 = ((f32[8,8,128]{2,1,0:T(8,128)}), f32[8,8,128]{2,1,0:T(8,128)S(1)}, u32[]{:S(2)}, u32[]{:S(2)}) async-start(f32[8,8,128]{2,1,0:T(8,128)} %force.1), calls=%async_computation.1 | async-start | bytes 65536 | tf_op jit(solution)/shard_map/all_to_all | solution.py:451
  36.1 0.0 copy-start.16
  36.1 0.7 fusion.3
  36.8 0.0 copy-done.16
  36.8 0.6 copy.49
  37.4 2.7 %all-to-all-done.1.msgs = f32[8,8,128]{2,1,0:T(8,128)S(1)} async-done(((f32[8,8,128]{2,1,0:T(8,128)}), f32[8,8,128]{2,1,0:T(8,128)S(1)}, u32[]{:S(2)}, u32[]{:S(2)}) %all-to-all-start.1) | async-done | bytes 32800 | tf_op jit(solution)/shard_map/all_to_all | solution.py:451
  40.1 0.0 copy-start.12
  40.1 0.6 copy-done.12
  40.7 1.6 %kick.1 = (f32[3,128]{1,0:T(4,128)}, f32[3,128]{1,0:T(4,128)}) custom-call(f32[8,8,128]{2,1,0:T(8,128)} %copy-done.12, f32[3,128]{1,0:T(4,128)} %bitcast.34, s32[1,128]{1,0:T(1,128)} %bitcast.36, s32[1,128]{1,0:T(1,128)} %halo.3), custom_call_target="tpu_custom_call" | custom-call | tf_op jit(solution)/shard_map/kick/pallas_call | solution.py:452
  42.4 0.0 copy-start.14
  42.4 0.0 copy-start.13
  42.4 0.7 copy-done.14
  43.0 0.0 copy-done.13
  43.1 0.1 multiply_add_fusion.1
  43.2 0.8 %copy.41 = f32[64,2,3,128]{3,1,2,0:T(2,128)} copy(f32[64,2,3,128]{3,0,2,1:T(8,128)S(1)} %pad_maximum_fusion) | data formatting | bytes 393216 | tf_op jit(solution)/shard_map/stack | solution.py:460
  44.0 14.4 %all-to-all-start.2 = ((f32[64,2,3,128]{3,1,2,0:T(2,128)}), f32[64,2,3,128]{3,1,2,0:T(2,128)S(1)}, u32[]{:S(2)}, u32[]{:S(2)}) async-start(f32[64,2,3,128]{3,1,2,0:T(2,128)} %copy.41), calls=%async_computation.2 | async-start | bytes 393216 | tf_op jit(solution)/shard_map/all_to_all | solution.py:467
  58.4 0.0 copy-start.15
  58.4 0.7 copy-done.15
  59.1 0.6 copy.42
  59.6 18.9 %all-to-all-done.2 = f32[64,2,3,128]{3,1,2,0:T(2,128)S(1)} async-done(((f32[64,2,3,128]{3,1,2,0:T(2,128)}), f32[64,2,3,128]{3,1,2,0:T(2,128)S(1)}, u32[]{:S(2)}, u32[]{:S(2)}) %all-to-all-start.2) | async-done | bytes 196640 | tf_op jit(solution)/shard_map/all_to_all | solution.py:467
  78.6 0.1 reduce_sum.9
  78.7 0.6 slice_bitcast_fusion
  (5 shorter events, 0.1 us)
Async XLA Ops:
  0.6 15.0 %copy-start.11 = (bf16[1600,240]{0,1:T(8,128)(2,1)S(1)}, bf16[1600,240]{0,1:T(8,128)(2,1)}, u32[]{:S(2)}) copy-start(bf16[1600,240]{0,1:T(8,128)(2,1)} %param.40) | copy-start | bytes 2304004
  6.5 13.5 %all-to-all-start = ((f32[8,24,128]{2,1,0:T(8,128)}), f32[8,24,128]{2,1,0:T(8,128)S(1)}, u32[]{:S(2)}, u32[]{:S(2)}) async-start(f32[8,24,128]{2,1,0:T(8,128)} %pad_maximum_fusion.1), calls=%async_computation | async-start | bytes 196608 | tf_op jit(solution)/shard_map/all_to_all | solution.py:445
  15.7 4.5 %copy-start = (bf16[1664,128]{1,0:T(8,128)(2,1)S(1)}, bf16[1664,128]{1,0:T(8,128)(2,1)}, u32[]{:S(2)}) copy-start(bf16[1664,128]{1,0:T(8,128)(2,1)} %constant.72.clone.fold_hbm) | copy-start | bytes 1277956
  15.7 4.5 %copy-start.2 = (bf16[240,240]{1,0:T(8,128)(2,1)S(1)}, bf16[240,240]{1,0:T(8,128)(2,1)}, u32[]{:S(2)}) copy-start(bf16[240,240]{1,0:T(8,128)(2,1)} %fit3_hbm.1) | copy-start | bytes 345604
  15.7 4.5 %copy-start.5 = (bf16[56,32]{1,0:T(8,128)(2,1)S(1)}, bf16[56,32]{1,0:T(8,128)(2,1)}, u32[]{:S(2)}) copy-start(bf16[56,32]{1,0:T(8,128)(2,1)} %get-tuple-element.10.w2t) | copy-start | bytes 10756
  15.7 4.5 %copy-start.6 = (s32[16,128]{1,0:T(8,128)S(1)}, s32[16,128]{1,0:T(8,128)}, u32[]{:S(2)}) copy-start(s32[16,128]{1,0:T(8,128)} %constant.71.clone.spread) | copy-start | bytes 24580
  16.5 3.7 %copy-start.1 = (bf16[240,240]{1,0:T(8,128)(2,1)S(1)}, bf16[240,240]{1,0:T(8,128)(2,1)}, u32[]{:S(2)}) copy-start(bf16[240,240]{1,0:T(8,128)(2,1)} %fit2_hbm.1) | copy-start | bytes 345604
  20.0 0.7 copy-start.4
  20.1 0.8 %copy-start.3 = (f32[4,32,128]{2,1,0:T(8,128)S(1)}, f32[4,32,128]{2,1,0:T(8,128)}, u32[]{:S(2)}) copy-start(f32[4,32,128]{2,1,0:T(8,128)} %get-tuple-element.12.cols) | copy-start | bytes 196612
  20.1 0.8 %copy-start.9 = (f32[240]{0:T(256)S(1)}, f32[240]{0:T(256)}, u32[]{:S(2)}) copy-start(f32[240]{0:T(256)} %param.43) | copy-start | bytes 2884
  20.1 0.8 %copy-start.10 = (f32[240]{0:T(256)S(1)}, f32[240]{0:T(256)}, u32[]{:S(2)}) copy-start(f32[240]{0:T(256)} %param.45) | copy-start | bytes 2884
  20.1 0.8 %copy-start.7 = (f32[2,240]{1,0:T(2,128)S(1)}, f32[2,240]{1,0:T(2,128)}, u32[]{:S(2)}) copy-start(f32[2,240]{1,0:T(2,128)} %readout.1) | copy-start | bytes 5764
  20.1 0.8 %copy-start.8 = (f32[240]{0:T(256)S(1)}, f32[240]{0:T(256)}, u32[]{:S(2)}) copy-start(f32[240]{0:T(256)} %param.41) | copy-start | bytes 2884
  31.4 8.7 %all-to-all-start.1 = ((f32[8,8,128]{2,1,0:T(8,128)}), f32[8,8,128]{2,1,0:T(8,128)S(1)}, u32[]{:S(2)}, u32[]{:S(2)}) async-start(f32[8,8,128]{2,1,0:T(8,128)} %force.1), calls=%async_computation.1 | async-start | bytes 65536 | tf_op jit(solution)/shard_map/all_to_all | solution.py:451
  36.1 0.7 copy-start.16
  40.1 0.6 copy-start.12
  42.4 0.7 copy-start.14
  42.4 0.7 copy-start.13
  44.0 34.6 %all-to-all-start.2 = ((f32[64,2,3,128]{3,1,2,0:T(2,128)}), f32[64,2,3,128]{3,1,2,0:T(2,128)S(1)}, u32[]{:S(2)}, u32[]{:S(2)}) async-start(f32[64,2,3,128]{3,1,2,0:T(2,128)} %copy.41), calls=%async_computation.2 | async-start | bytes 393216 | tf_op jit(solution)/shard_map/all_to_all | solution.py:467
  58.4 0.7 copy-start.15

commit v2 on v1

--- a/solution.py
+++ b/solution.py
@@ -399,21 +399,152 @@
     )
 
 
-def prepare_kernel(pos, types, halo, scale, shift, w2, b2, w3, b3, s1, a2, p1, a3, p2, tile, w2t, w3t, cols):
-    tile[...] = own_tile(pos[...], types[...], halo[...])
+MESH = pl.DeviceIdType.MESH
+NZ = 16
+NY = 4
+REACH = 4
+
+
+def greet(peers):
+    barrier = pltpu.get_barrier_semaphore()
+    for peer in peers:
+        pl.semaphore_signal(barrier, inc=1, device_id=peer, device_id_type=MESH)
+    pl.semaphore_wait(barrier, len(peers))
+
+
+def send(src, dst, out_sem, in_sem, peer):
+    copy = pltpu.make_async_remote_copy(
+        src_ref=src, dst_ref=dst, send_sem=out_sem, recv_sem=in_sem, device_id=peer, device_id_type=MESH
+    )
+    copy.start()
+    return copy
+
+
+def slab_peers():
+    me = lax.axis_index("slab")
+    return me, [{"slab": lax.rem(me + i, N_SLAB)} for i in range(1, N_SLAB)]
+
+
+def exchange_kernel(
+    pos, types, halo, lists, scale, shift, w2, b2, w3, b3, s1, a2, p1, a3, p2,
+    tiles, nb, w2t, w3t, cols,
+    tile_out, tile_in, list_out, list_in, own_sem,
+):
+    me, peers = slab_peers()
+    tiles[me] = own_tile(pos[...], types[...], halo[...])
+    greet(peers)
+    copies = []
+    for i, peer in enumerate(peers):
+        copies.append(send(lists.at[:, i + 1, :], nb.at[me], list_out.at[i], list_in.at[i], peer))
+    for i, peer in enumerate(peers):
+        copies.append(send(tiles.at[me], tiles.at[me], tile_out.at[i], tile_in.at[i], peer))
+    own = pltpu.make_async_copy(lists.at[:, 0, :], nb.at[me], own_sem)
+    own.start()
     prepare_weights(scale, shift, w2, b2, w3, b3, s1, a2, p1, a3, p2, w2t, w3t, cols)
-
-
-def kick_kernel(msgs, vel, types, halo, forces, kicked):
-    got = msgs[0]
-    for s in range(1, N_SLAB):
-        got = got + msgs[s]
+    own.wait()
+    for copy in copies:
+        copy.wait()
+
+
+def finish_kernel(
+    msgs, pos, vel, types, halo, coefs,
+    pos_out, vel_out, force_out,
+    inbox, ring, mixed, ybox, slab_out, slab_in, ring_out, ring_in, far_out, far_in, y_out, y_in,
+):
+    me, peers = slab_peers()
+    bead = lax.axis_index("bead")
+    z, y = lax.div(bead, NY), lax.rem(bead, NY)
+
+    def along(d):
+        return {"bead": lax.rem(z + NZ + d, NZ) * NY + y}
+
+    steps = [d for k in range(1, REACH + 1) for d in (k, -k)]
+    yet = [lax.rem(y + k, NY) for k in range(1, NY)]
+    ypeers = [{"bead": z * NY + other} for other in yet]
+    greet(peers + [along(d) for d in steps] + ypeers)
+
+    copies = [
+        send(msgs.at[lax.rem(me + i + 1, N_SLAB)], inbox.at[i], slab_out.at[i], slab_in.at[i], peer)
+        for i, peer in enumerate(peers)
+    ]
     bins = pltpu.roll(spread_rows(halo[...], 8), 64, 1)[0:1]
     hit = jnp.where(lax.broadcasted_iota(jnp.int32, (LANES, LANES), 0) == bins, 1.0, 0.0)
+    got = msgs[me]
+    for i, copy in enumerate(copies):
+        copy.wait()
+        got = got + inbox[i]
     back = lax.dot_general(got, hit, NT, preferred_element_type=F32, precision=HIGH)
     force = -(got[0:3] + back[3:6])
-    forces[...] = force
-    kicked[...] = vel[...] + STEP * jnp.where(types[...] == 1, 1.0, 1.0 / HEAVY) * force
+    kicked = vel[...] + STEP * jnp.where(types[...] == 1, 1.0, 1.0 / HEAVY) * force
+    own = ring.at[8]
+    own[...] = jnp.concatenate([pos[...], kicked, jnp.zeros((2, LANES), F32)], axis=0)
+
+    near = {
+        d: send(own, ring.at[8 - d], ring_out.at[n], ring_in.at[n], along(d)) for n, d in enumerate(steps)
+    }
+    force_out[...] = force
+    for d in steps:
+        if d > 0:
+            near[d].wait_recv()
+    up = send(ring.at[pl.ds(4, 4)], ring.at[pl.ds(0, 4)], far_out.at[0], far_in.at[0], along(REACH))
+    for d in steps:
+        if d < 0:
+            near[d].wait_recv()
+    down = send(ring.at[pl.ds(9, 3)], ring.at[pl.ds(13, 3)], far_out.at[1], far_in.at[1], along(-REACH))
+    for d in steps:
+        near[d].wait_send()
+    up.wait()
+    down.wait()
+
+    blocks = jnp.concatenate([ring[n] for n in range(NZ)], axis=0)
+    sums = lax.dot_general(
+        coefs[y], blocks, (((1,), (0,)), ((), ())), preferred_element_type=F32, precision=HIGH
+    )
+    for k in range(NY):
+        mixed[k] = sums[8 * k : 8 * k + 8]
+    copies = [
+        send(mixed.at[other], ybox.at[i], y_out.at[i], y_in.at[i], peer)
+        for i, (other, peer) in enumerate(zip(yet, ypeers))
+    ]
+    done = mixed[y]
+    for i, copy in enumerate(copies):
+        copy.wait()
+        done = done + ybox[i]
+    pos_out[...] = done[0:3]
+    vel_out[...] = done[3:6]
+
+
+def ring_coefficients():
+    cos, travel, spring = (m[:, 0].astype(np.float64) for m in mode_matrices())
+    table = np.zeros((NY, NY, 8, NZ, 8), np.float32)
+    for y in range(NY):
+        for to in range(NY):
+            for slot in range(NZ):
+                apart = (to - y - NY * (slot - 8)) % BEADS
+                for c in range(3):
+                    table[y, to, c, slot, c] = cos[apart]
+                    table[y, to, c, slot, 3 + c] = travel[apart]
+                    table[y, to, 3 + c, slot, c] = -spring[apart]
+                    table[y, to, 3 + c, slot, 3 + c] = cos[apart]
+    return table.reshape(NY, NY * 8, NZ * 8)
+
+
+def finish_call(msgs, pos, vel, types, halo):
+    dma = lambda n: pltpu.SemaphoreType.DMA((n,))
+    near = 2 * REACH
+    return pl.pallas_call(
+        finish_kernel,
+        out_shape=(jax.ShapeDtypeStruct((3, LANES), F32),) * 3,
+        scratch_shapes=[
+            pltpu.VMEM((7, 8, LANES), F32),
+            pltpu.VMEM((NZ, 8, LANES), F32),
+            pltpu.VMEM((NY, 8, LANES), F32),
+            pltpu.VMEM((NY - 1, 8, LANES), F32),
+            dma(7), dma(7), dma(near), dma(near), dma(2), dma(2), dma(NY - 1), dma(NY - 1),
+        ],
+        compiler_params=pltpu.CompilerParams(collective_id=1, has_side_effects=True),
+        name="finish",
+    )(msgs, pos, vel, types, halo, jnp.asarray(ring_coefficients()))
 
 
 def local(
@@ -424,51 +555,33 @@
     del live_atoms
     pos, vel, types = positions[:, 0, :], velocities[:, 0, :], atom_types[None]
     s1, a2, p1, a3, p2, _, _ = selections()
-    tile, w2t, w3t, cols = pl.pallas_call(
-        prepare_kernel,
+    dma = lambda n: pltpu.SemaphoreType.DMA((n,))
+    vm = pl.BlockSpec(memory_space=pltpu.VMEM)
+    tiles, nb, w2t, w3t, cols = pl.pallas_call(
+        exchange_kernel,
         out_shape=(
-            jax.ShapeDtypeStruct((8, LANES), F32),
+            jax.ShapeDtypeStruct((N_SLAB, 8, LANES), F32),
+            jax.ShapeDtypeStruct((N_SLAB, SHARE, LANES), jnp.int32),
             jax.ShapeDtypeStruct((56, 32), BF16),
             jax.ShapeDtypeStruct((104, 56), BF16),
             jax.ShapeDtypeStruct((4, 32, LANES), F32),
         ),
-        name="prepare",
+        in_specs=[vm] * 3 + [pl.BlockSpec(memory_space=pl.ANY)] + [vm] * 11,
+        out_specs=(vm,) * 5,
+        scratch_shapes=[dma(7), dma(7), dma(7), dma(7), pltpu.SemaphoreType.DMA],
+        compiler_params=pltpu.CompilerParams(collective_id=0, has_side_effects=True),
+        name="exchange",
     )(
-        pos, types, halo_rows, type_scale, type_shift, embed_two, embed_bias_two[None],
-        embed_three, embed_bias_three[None], jnp.asarray(s1), jnp.asarray(a2, BF16),
-        jnp.asarray(p1, BF16), jnp.asarray(a3, BF16), jnp.asarray(p2, BF16),
-    )
-    me = lax.axis_index("slab")
-    dealt = jnp.moveaxis(neighbours.reshape(SHARE, N_SLAB, LANES), 1, 0).astype(F32)
-    dealt = jnp.roll(dealt, me, axis=0)
-    parcel = jnp.concatenate([jnp.broadcast_to(tile, (N_SLAB, 8, LANES)), dealt], axis=1)
-    parcel = lax.all_to_all(parcel, "slab", 0, 0, tiled=True)
-    nb = parcel[:, 8:].astype(jnp.int32)
+        pos, types, halo_rows, neighbours.reshape(SHARE, N_SLAB, LANES), type_scale, type_shift,
+        embed_two, embed_bias_two[None], embed_three, embed_bias_three[None], jnp.asarray(s1),
+        jnp.asarray(a2, BF16), jnp.asarray(p1, BF16), jnp.asarray(a3, BF16), jnp.asarray(p2, BF16),
+    )
     msgs = force_call(
-        parcel[:, :8], nb, w2t, w3t, cols,
+        tiles, nb, w2t, w3t, cols,
         (fit_first, fit_bias_first, fit_second, fit_bias_second, fit_third, fit_bias_third, fit_readout),
     )
-    msgs = lax.all_to_all(msgs, "slab", 0, 0, tiled=True)
-    forces, kicked = pl.pallas_call(
-        kick_kernel,
-        out_shape=(jax.ShapeDtypeStruct((3, LANES), F32),) * 2,
-        name="kick",
-    )(msgs, vel, types, halo_rows)
-    own = lax.axis_index("bead")
-    cos, travel, spring = (jnp.asarray(m) for m in mode_matrices())
-    col = lambda m: lax.dynamic_index_in_dim(m, own, 1, keepdims=False)[:BEADS_HERE, None, None]
-    mixed = jnp.stack(
-        [
-            col(cos) * pos + col(travel) * kicked,
-            col(-spring) * pos + col(cos) * kicked,
-        ],
-        axis=1,
-    )
-    mixed = lax.all_to_all(mixed, "bead", 0, 0, tiled=True).sum(axis=0)
-    return mixed[0][:, None, :], mixed[1][:, None, :], forces[:, None, :]
-
-
-BEADS_HERE = BEADS
+    outs = finish_call(msgs, pos, vel, types, halo_rows)
+    return tuple(out[:, None, :] for out in outs)
 
 
 def solution(mesh):

time: 79.9 us -> 57.9 us (0.72)
  the two profiles are of different devices: /device:TPU:2 before, /device:TPU:1 now
where the time goes in v2:
time: 57.9 us; the launch traced here: 57.3 us
  Pallas kernels  50.3 us (87%)
  local copies, waits for them, and re-layouts  6.12 us (11%)
  between operations  0.9 us (2%)
    pallas_call x1, Pallas kernels, finish_call(): pl.pallas_call(finish_kernel, out_shape=(jax.ShapeDtypeStruct((3, LANES),...  24.8 us
    pallas_call x1, Pallas kernels, local(): pl.pallas_call(exchange_kernel, out_shape=(jax.ShapeDtypeStruct((N_SLAB,...  14.8 us
    pallas_call x1, Pallas kernels, force_call(): pl.pallas_call(force_kernel, out_shape=jax.ShapeDtypeStruct((N_SLAB, 8, L...  10.6 us
    unnamed x43, local copies, waits for them, and re-layouts  6.12 us

profile of v2, /device:TPU:1, one launch (start us, length us, event | category | flops | bytes accessed | tf_op | source)
XLA Modules:
  0.0 57.3 jit_solution(3914374792672900578)
XLA Ops:
  0.6 0.0 copy-start.17
  0.6 0.0 copy-start.18
  0.6 0.7 %copy-done.17 = f32[3,1,128]{2,1,0:T(1,128)S(1)} copy-done((f32[3,1,128]{2,1,0:T(1,128)S(1)}, f32[3,1,128]{2,1,0:T(1,128)}, u32[]{:S(2)}) %copy-start.17) | copy-done | bytes 1560
  1.3 0.0 copy-done.18
  1.3 0.6 %copy_bitcast_fusion = (f32[3,128]{1,0:T(4,128)}, f32[3,128]{1,0:T(4,128)}) fusion(f32[3,1,128]{2,1,0:T(1,128)S(1)} %copy-done.17, f32[3,1,128]{2,1,0:T(1,128)S(1)} %copy-done.18), kind=kLoop, calls=%fused_computation | loop fusion | bytes 6144
  1.9 14.8 %exchange.1 = (f32[8,8,128]{2,1,0:T(8,128)}, s32[8,16,128]{2,1,0:T(8,128)}, bf16[56,32]{1,0:T(8,128)(2,1)}, bf16[104,56]{1,0:T(8,128)(2,1)}, f32[4,32,128]{2,1,0:T(8,128)}) custom-call(f32[3,128]{1,0:T(4,128)} %get-tuple-element.23.pos, s32[1,128]{1,0:T(1,128)} %bitcast.18, s32[1,128]{1,0:T(1,128)} %halo.3, s32[16,8,128]{2,1,0:T(8,128)} %bitcast.17, ...), custom_call_target="tpu_custom_call" | custom-call | tf_op jit(solution)/shard_map/exchange/pallas_call | solution.py:560
  16.7 0.0 copy-start
  16.7 0.0 copy-start.2
  16.8 0.0 copy-start.3
  16.8 0.0 copy-start.4
  16.8 0.0 copy-start.5
  16.8 0.0 copy-start.6
  16.8 0.0 copy-start.7
  16.8 0.0 copy-start.8
  16.8 0.0 copy-start.9
  16.8 0.0 copy-start.10
  16.8 0.0 copy-start.11
  16.9 0.0 copy-start.12
  16.9 0.0 copy-start.13
  16.9 1.6 %copy.29.fit1_hbm = bf16[1600,240]{1,0:T(8,128)(2,1)S(1)} copy(bf16[1600,240]{0,1:T(8,128)(2,1)} %param.38) | data formatting | bytes 1536000 | tf_op args[12]
  18.5 0.0 copy-done
  18.5 0.0 copy-done.2
  18.5 0.0 copy-done.3
  18.5 0.0 copy-done.4
  18.5 0.0 copy-done.5
  18.6 0.0 copy-done.6
  18.6 0.0 copy-done.7
  18.6 0.0 copy-done.8
  18.6 0.0 copy-done.9
  18.6 0.0 copy-done.10
  18.6 0.0 copy-done.11
  18.6 0.0 copy-done.12
  18.6 0.0 copy-done.13
  18.6 10.6 %force.1.msgs = f32[8,8,128]{2,1,0:T(8,128)S(1)} custom-call(f32[8,8,128]{2,1,0:T(8,128)S(1)} %copy-done.6, s32[8,16,128]{2,1,0:T(8,128)S(1)} %copy-done.4, bf16[56,32]{1,0:T(8,128)(2,1)S(1)} %copy-done.8, bf16[104,56]{1,0:T(8,128)(2,1)S(1)} %copy-done.7, f32[4,32,128]{2,1,0:T(8,128)S(1)} %copy-done.5, s32[16,128]{1,0:T(8,128)S(1)} %copy-done.9, ...), custom_call_target="tpu_custom_call" | custom-call | tf_op jit(solution)/shard_map/force/pallas_call | solution.py:371
  29.3 0.0 copy-start.1
  29.3 0.6 %copy-done.1 = f32[8,8,128]{2,1,0:T(8,128)} copy-done((f32[8,8,128]{2,1,0:T(8,128)}, f32[8,8,128]{2,1,0:T(8,128)S(1)}, u32[]{:S(2)}) %copy-start.1) | copy-done | bytes 32792
  29.9 24.8 %finish.1 = (f32[3,128]{1,0:T(4,128)}, f32[3,128]{1,0:T(4,128)}, f32[3,128]{1,0:T(4,128)}) custom-call(f32[8,8,128]{2,1,0:T(8,128)} %copy-done.1, f32[3,128]{1,0:T(4,128)} %get-tuple-element.23.pos, f32[3,128]{1,0:T(4,128)} %get-tuple-element.22.vel, s32[1,128]{1,0:T(1,128)} %bitcast.19, s32[1,128]{1,0:T(1,128)} %halo.3, f32[4,32,128]{2,1,0:T(8,128)} %constant.23.clone.coefs), custom_call_target="tpu_custom_call" | custom-call | tf_op jit(solution)/shard_map/finish/pallas_call | solution.py:535
  54.7 0.0 copy-start.16
  54.7 0.7 %copy-done.16 = f32[3,128]{1,0:T(4,128)S(1)} copy-done((f32[3,128]{1,0:T(4,128)S(1)}, f32[3,128]{1,0:T(4,128)}, u32[]{:S(2)}) %copy-start.16) | copy-done | bytes 1560
  55.4 0.0 copy-start.15
  55.4 0.6 copy.30
  55.9 0.1 copy-done.15
  56.0 0.0 copy-start.14
  56.0 0.6 copy.31
  56.6 0.1 copy-done.14
  56.7 0.6 copy.32
Async XLA Ops:
  0.6 0.7 %copy-start.17 = (f32[3,1,128]{2,1,0:T(1,128)S(1)}, f32[3,1,128]{2,1,0:T(1,128)}, u32[]{:S(2)}) copy-start(f32[3,1,128]{2,1,0:T(1,128)} %param.28) | copy-start | bytes 4612
  0.6 0.7 %copy-start.18 = (f32[3,1,128]{2,1,0:T(1,128)S(1)}, f32[3,1,128]{2,1,0:T(1,128)}, u32[]{:S(2)}) copy-start(f32[3,1,128]{2,1,0:T(1,128)} %param.27) | copy-start | bytes 4612
  16.7 1.8 %copy-start = (bf16[1664,128]{1,0:T(8,128)(2,1)S(1)}, bf16[1664,128]{1,0:T(8,128)(2,1)}, u32[]{:S(2)}) copy-start(bf16[1664,128]{1,0:T(8,128)(2,1)} %constant.22.clone.fold_hbm) | copy-start | bytes 1277956
  16.7 1.8 %copy-start.2 = (bf16[240,240]{1,0:T(8,128)(2,1)S(1)}, bf16[240,240]{1,0:T(8,128)(2,1)}, u32[]{:S(2)}) copy-start(bf16[240,240]{1,0:T(8,128)(2,1)} %fit2_hbm.1) | copy-start | bytes 345604
  16.8 1.8 %copy-start.3 = (bf16[240,240]{1,0:T(8,128)(2,1)S(1)}, bf16[240,240]{1,0:T(8,128)(2,1)}, u32[]{:S(2)}) copy-start(bf16[240,240]{1,0:T(8,128)(2,1)} %fit3_hbm.1) | copy-start | bytes 345604
  16.8 1.8 %copy-start.4 = (s32[8,16,128]{2,1,0:T(8,128)S(1)}, s32[8,16,128]{2,1,0:T(8,128)}, u32[]{:S(2)}) copy-start(s32[8,16,128]{2,1,0:T(8,128)} %get-tuple-element.12.nb) | copy-start | bytes 196612
  16.8 1.8 %copy-start.5 = (f32[4,32,128]{2,1,0:T(8,128)S(1)}, f32[4,32,128]{2,1,0:T(8,128)}, u32[]{:S(2)}) copy-start(f32[4,32,128]{2,1,0:T(8,128)} %get-tuple-element.15.cols) | copy-start | bytes 196612
  16.8 1.8 %copy-start.6 = (f32[8,8,128]{2,1,0:T(8,128)S(1)}, f32[8,8,128]{2,1,0:T(8,128)}, u32[]{:S(2)}) copy-start(f32[8,8,128]{2,1,0:T(8,128)} %get-tuple-element.11.tile) | copy-start | bytes 98308
  16.8 1.8 %copy-start.7 = (bf16[104,56]{1,0:T(8,128)(2,1)S(1)}, bf16[104,56]{1,0:T(8,128)(2,1)}, u32[]{:S(2)}) copy-start(bf16[104,56]{1,0:T(8,128)(2,1)} %get-tuple-element.14.w3t) | copy-start | bytes 34948
  16.8 1.8 %copy-start.8 = (bf16[56,32]{1,0:T(8,128)(2,1)S(1)}, bf16[56,32]{1,0:T(8,128)(2,1)}, u32[]{:S(2)}) copy-start(bf16[56,32]{1,0:T(8,128)(2,1)} %get-tuple-element.13.w2t) | copy-start | bytes 10756
  16.8 1.8 %copy-start.9 = (s32[16,128]{1,0:T(8,128)S(1)}, s32[16,128]{1,0:T(8,128)}, u32[]{:S(2)}) copy-start(s32[16,128]{1,0:T(8,128)} %constant.21.clone.spread) | copy-start | bytes 24580
  16.8 1.8 %copy-start.10 = (f32[2,240]{1,0:T(2,128)S(1)}, f32[2,240]{1,0:T(2,128)}, u32[]{:S(2)}) copy-start(f32[2,240]{1,0:T(2,128)} %readout.1) | copy-start | bytes 5764
  16.8 1.8 %copy-start.11 = (f32[240]{0:T(256)S(1)}, f32[240]{0:T(256)}, u32[]{:S(2)}) copy-start(f32[240]{0:T(256)} %param.39) | copy-start | bytes 2884
  16.9 1.8 %copy-start.12 = (f32[240]{0:T(256)S(1)}, f32[240]{0:T(256)}, u32[]{:S(2)}) copy-start(f32[240]{0:T(256)} %param.41) | copy-start | bytes 2884
  16.9 1.8 %copy-start.13 = (f32[240]{0:T(256)S(1)}, f32[240]{0:T(256)}, u32[]{:S(2)}) copy-start(f32[240]{0:T(256)} %param.43) | copy-start | bytes 2884
  29.3 0.6 %copy-start.1 = (f32[8,8,128]{2,1,0:T(8,128)}, f32[8,8,128]{2,1,0:T(8,128)S(1)}, u32[]{:S(2)}) copy-start(f32[8,8,128]{2,1,0:T(8,128)S(1)} %force.1.msgs) | copy-start | bytes 98308
  54.7 0.7 %copy-start.16 = (f32[3,128]{1,0:T(4,128)S(1)}, f32[3,128]{1,0:T(4,128)}, u32[]{:S(2)}) copy-start(f32[3,128]{1,0:T(4,128)} %get-tuple-element.16) | copy-start | bytes 4612
  55.4 0.7 %copy-start.15 = (f32[3,128]{1,0:T(4,128)S(1)}, f32[3,128]{1,0:T(4,128)}, u32[]{:S(2)}) copy-start(f32[3,128]{1,0:T(4,128)} %get-tuple-element.17) | copy-start | bytes 4612
  56.0 0.7 %copy-start.14 = (f32[3,128]{1,0:T(4,128)S(1)}, f32[3,128]{1,0:T(4,128)}, u32[]{:S(2)}) copy-start(f32[3,128]{1,0:T(4,128)} %get-tuple-element.18) | copy-start | bytes 4612

commit v3 on v2

--- a/solution.py
+++ b/solution.py
@@ -20,6 +20,7 @@
 BF16 = jnp.bfloat16
 NT = (((1,), (1,)), ((), ()))
 HIGH = lax.Precision.HIGHEST
+PLACE = pltpu.HBM
 
 
 def two_feature(row):
@@ -146,20 +147,23 @@
             cols[2 * n + kind] = col + ones if n else col
 
 
-def force_kernel(
-    tile, nb, w2t, w3t, cols, spread, fold_hbm, fit1_hbm, fit2_hbm, fit3_hbm, c1, c2, c3, readout,
-    out,
-    env, geo, order, count, hc, three, feats, gfeats, qs, ps, scat, fold, fit1, fit2, fit3, sems,
-):
-    me = lax.axis_index("slab")
-    loads = [
-        pltpu.make_async_copy(src, dst, sems.at[n])
-        for n, (src, dst) in enumerate(
-            ((fit1_hbm, fit1), (fit2_hbm, fit2), (fit3_hbm, fit3), (fold_hbm, fold))
-        )
-    ]
+def fetch(pairs, sems, first=0):
+    loads = [pltpu.make_async_copy(src, dst, sems.at[first + n]) for n, (src, dst) in enumerate(pairs)]
     for load in loads:
         load.start()
+    return loads
+
+
+def force_kernel(*refs):
+    given, out, held, rest = refs[:14], refs[14], refs[15:29], refs[29:]
+    (
+        tile, nb, w2t, w3t, cols, spread, c1, c2, c3, readout, fit1, fit2, fit3, fold,
+    ) = held
+    env, geo, order, count, hc, three, feats, gfeats, qs, ps, scat, sems = rest
+    me = lax.axis_index("slab")
+    loads = fetch(list(zip(given, held)), sems)
+    for load in loads[:2]:
+        load.wait()
     dot = functools.partial(lax.dot_general, preferred_element_type=F32)
     NN = (((1,), (0,)), ((), ()))
     lane8 = lax.broadcasted_iota(jnp.int32, (8, LANES), 1)
@@ -221,6 +225,8 @@
 
     second_half(geometry)
 
+    for load in loads[2:6]:
+        load.wait()
     sc0, sc1, sh0, sh1 = 0, 1, 2, 3
 
     def forward(block, carry):
@@ -264,7 +270,7 @@
     blocks = lax.div(total + (BLK - 1), BLK)
     lax.fori_loop(0, blocks, forward, 0)
 
-    for load in loads:
+    for load in loads[6:]:
         load.wait()
 
     lane_m = lax.broadcasted_iota(jnp.int32, (CHUNK, LANES), 1)
@@ -278,7 +284,7 @@
         ]
         desc = [sum(spreads[g][c] * tiled[c] for c in range(4)) for g in range(13)]
         desc = jnp.concatenate(desc, axis=1).astype(BF16)[:, :1600]
-        f1 = jnp.tanh(dot(desc, fit1[...], NN) + c1[...])
+        f1 = jnp.tanh(dot(desc, fit1[...], NT) + c1[...])
         t2 = jnp.tanh(dot(f1.astype(BF16), fit2[...], NN) + c2[...])
         f2 = t2 + f1
         t3 = jnp.tanh(dot(f2.astype(BF16), fit3[...], NN) + c3[...])
@@ -287,7 +293,7 @@
         g3 = readout[0:1, :] + h * (readout[1:2, :] - readout[0:1, :])
         g2 = g3 + dot((g3 * (1.0 - t3 * t3)).astype(BF16), fit3[...], NT)
         g1 = g2 + dot((g2 * (1.0 - t2 * t2)).astype(BF16), fit2[...], NT)
-        gd = dot((g1 * (1.0 - f1 * f1)).astype(BF16), fit1[...], NT)
+        gd = dot((g1 * (1.0 - f1 * f1)).astype(BF16), fit1[...], NN)
         gd = jnp.concatenate([gd, jnp.zeros((CHUNK, 64), F32)], axis=1)
         parts = [gd[:, g * LANES : (g + 1) * LANES] for g in range(13)]
         for c in range(4):
@@ -366,14 +372,16 @@
     fit1, b1, fit2, b2, fit3, b3, readout = fit
     _, _, _, _, _, spread, fold = selections()
     rows = N_SLAB * SHARE
-    vm = pl.BlockSpec(memory_space=pltpu.VMEM)
-    anyw = pl.BlockSpec(memory_space=pl.ANY)
+    operands = (
+        tile, nb, w2t, w3t, cols, jnp.asarray(spread), b1[None], b2[None], b3[None], readout,
+        fit1.T, fit2, fit3, jnp.asarray(fold, BF16),
+    )
     return pl.pallas_call(
         force_kernel,
         out_shape=jax.ShapeDtypeStruct((N_SLAB, 8, LANES), F32),
-        in_specs=[vm] * 6 + [anyw] * 4 + [vm] * 4,
-        out_specs=vm,
-        scratch_shapes=[
+        in_specs=[pl.BlockSpec(memory_space=PLACE)] * len(operands),
+        out_specs=pl.BlockSpec(memory_space=pltpu.VMEM),
+        scratch_shapes=[pltpu.VMEM(x.shape, x.dtype) for x in operands] + [
             pltpu.VMEM(((rows + 1) * 8, LANES), F32),
             pltpu.VMEM((5, rows, LANES), F32),
             pltpu.SMEM((rows + 24,), jnp.int32),
@@ -385,18 +393,10 @@
             pltpu.VMEM(((rows + 1) * 8, LANES), F32),
             pltpu.VMEM(((rows + 1) * 8, LANES), F32),
             pltpu.VMEM((rows * 8, LANES), F32),
-            pltpu.VMEM((13 * LANES, LANES), BF16),
-            pltpu.VMEM((1600, 240), BF16),
-            pltpu.VMEM((240, 240), BF16),
-            pltpu.VMEM((240, 240), BF16),
-            pltpu.SemaphoreType.DMA((4,)),
+            pltpu.SemaphoreType.DMA((len(operands),)),
         ],
-        compiler_params=pltpu.CompilerParams(vmem_limit_bytes=48 << 20),
         name="force",
-    )(
-        tile, nb, w2t, w3t, cols, jnp.asarray(spread), jnp.asarray(fold, BF16),
-        fit1, fit2, fit3, b1[None], b2[None], b3[None], readout,
-    )
+    )(*operands)
 
 
 MESH = pl.DeviceIdType.MESH
@@ -405,11 +405,14 @@
 REACH = 4
 
 
-def greet(peers):
+def hail(peers):
     barrier = pltpu.get_barrier_semaphore()
     for peer in peers:
         pl.semaphore_signal(barrier, inc=1, device_id=peer, device_id_type=MESH)
-    pl.semaphore_wait(barrier, len(peers))
+
+
+def meet(peers):
+    pl.semaphore_wait(pltpu.get_barrier_semaphore(), len(peers))
 
 
 def send(src, dst, out_sem, in_sem, peer):
@@ -425,31 +428,38 @@
     return me, [{"slab": lax.rem(me + i, N_SLAB)} for i in range(1, N_SLAB)]
 
 
-def exchange_kernel(
-    pos, types, halo, lists, scale, shift, w2, b2, w3, b3, s1, a2, p1, a3, p2,
-    tiles, nb, w2t, w3t, cols,
-    tile_out, tile_in, list_out, list_in, own_sem,
-):
+def exchange_kernel(*refs):
+    pos_in, types_in, halo_in, lists = refs[:4]
+    weights, (tiles, nb), results = refs[4:15], refs[15:17], refs[17:20]
+    pos, types, halo = refs[20:23]
+    held, made, mine = refs[23:34], refs[34:37], refs[37]
+    tile_out, tile_in, list_out, list_in, own_sems, load_sems = refs[38:]
     me, peers = slab_peers()
-    tiles[me] = own_tile(pos[...], types[...], halo[...])
-    greet(peers)
+    hail(peers)
+    first = fetch([(pos_in, pos), (types_in, types), (halo_in, halo)], load_sems)
+    later = fetch(list(zip(weights, held)), load_sems, 3)
+    for load in first:
+        load.wait()
+    mine[...] = own_tile(pos[:, 0, :], types[...], halo[...])
+    meet(peers)
     copies = []
     for i, peer in enumerate(peers):
         copies.append(send(lists.at[:, i + 1, :], nb.at[me], list_out.at[i], list_in.at[i], peer))
     for i, peer in enumerate(peers):
-        copies.append(send(tiles.at[me], tiles.at[me], tile_out.at[i], tile_in.at[i], peer))
-    own = pltpu.make_async_copy(lists.at[:, 0, :], nb.at[me], own_sem)
-    own.start()
-    prepare_weights(scale, shift, w2, b2, w3, b3, s1, a2, p1, a3, p2, w2t, w3t, cols)
-    own.wait()
-    for copy in copies:
+        copies.append(send(mine, tiles.at[me], tile_out.at[i], tile_in.at[i], peer))
+    own = fetch([(lists.at[:, 0, :], nb.at[me]), (mine, tiles.at[me])], own_sems)
+    for load in later:
+        load.wait()
+    prepare_weights(*held, *made)
+    own += fetch(list(zip(made, results)), own_sems, 2)
+    for copy in own + copies:
         copy.wait()
 
 
 def finish_kernel(
-    msgs, pos, vel, types, halo, coefs,
-    pos_out, vel_out, force_out,
-    inbox, ring, mixed, ybox, slab_out, slab_in, ring_out, ring_in, far_out, far_in, y_out, y_in,
+    msgs, pos_in, vel_in, types_in, halo_in, coefs_in, out,
+    mine, pos, vel, types, halo, coefs, inbox, ring, mixed, ybox, result,
+    slab_out, slab_in, ring_out, ring_in, far_out, far_in, y_out, y_in, load_sems,
 ):
     me, peers = slab_peers()
     bead = lax.axis_index("bead")
@@ -461,28 +471,39 @@
     steps = [d for k in range(1, REACH + 1) for d in (k, -k)]
     yet = [lax.rem(y + k, NY) for k in range(1, NY)]
     ypeers = [{"bead": z * NY + other} for other in yet]
-    greet(peers + [along(d) for d in steps] + ypeers)
+    everyone = [along(d) for d in steps[::-1]] + peers + ypeers
+    hail(everyone)
+    loads = fetch(
+        [
+            (msgs.at[me], mine), (pos_in, pos), (vel_in, vel), (types_in, types), (halo_in, halo),
+            (coefs_in.at[y], coefs),
+        ],
+        load_sems,
+    )
+    for load in loads:
+        load.wait()
+    bins = pltpu.roll(spread_rows(halo[...], 8), 64, 1)[0:1]
+    hit = jnp.where(lax.broadcasted_iota(jnp.int32, (LANES, LANES), 0) == bins, 1.0, 0.0)
+    meet(everyone)
 
     copies = [
         send(msgs.at[lax.rem(me + i + 1, N_SLAB)], inbox.at[i], slab_out.at[i], slab_in.at[i], peer)
         for i, peer in enumerate(peers)
     ]
-    bins = pltpu.roll(spread_rows(halo[...], 8), 64, 1)[0:1]
-    hit = jnp.where(lax.broadcasted_iota(jnp.int32, (LANES, LANES), 0) == bins, 1.0, 0.0)
-    got = msgs[me]
+    got = mine[...]
     for i, copy in enumerate(copies):
         copy.wait()
         got = got + inbox[i]
     back = lax.dot_general(got, hit, NT, preferred_element_type=F32, precision=HIGH)
     force = -(got[0:3] + back[3:6])
-    kicked = vel[...] + STEP * jnp.where(types[...] == 1, 1.0, 1.0 / HEAVY) * force
+    kicked = vel[:, 0, :] + STEP * jnp.where(types[...] == 1, 1.0, 1.0 / HEAVY) * force
     own = ring.at[8]
-    own[...] = jnp.concatenate([pos[...], kicked, jnp.zeros((2, LANES), F32)], axis=0)
+    own[...] = jnp.concatenate([pos[:, 0, :], kicked, jnp.zeros((2, LANES), F32)], axis=0)
 
     near = {
         d: send(own, ring.at[8 - d], ring_out.at[n], ring_in.at[n], along(d)) for n, d in enumerate(steps)
     }
-    force_out[...] = force
+    result[6:9, 0, :] = force
     for d in steps:
         if d > 0:
             near[d].wait_recv()
@@ -491,14 +512,17 @@
         if d < 0:
             near[d].wait_recv()
     down = send(ring.at[pl.ds(9, 3)], ring.at[pl.ds(13, 3)], far_out.at[1], far_in.at[1], along(-REACH))
+    NN = (((1,), (0,)), ((), ()))
+    dot = functools.partial(lax.dot_general, preferred_element_type=F32, precision=HIGH)
+    table = coefs[...]
+    sums = dot(table[:, 32:104], jnp.concatenate([ring[n] for n in range(4, 13)], axis=0), NN)
     for d in steps:
         near[d].wait_send()
     up.wait()
     down.wait()
-
-    blocks = jnp.concatenate([ring[n] for n in range(NZ)], axis=0)
-    sums = lax.dot_general(
-        coefs[y], blocks, (((1,), (0,)), ((), ())), preferred_element_type=F32, precision=HIGH
+    rest = [ring[n] for n in (0, 1, 2, 3, 13, 14, 15)]
+    sums = sums + dot(
+        jnp.concatenate([table[:, :32], table[:, 104:]], axis=1), jnp.concatenate(rest, axis=0), NN
     )
     for k in range(NY):
         mixed[k] = sums[8 * k : 8 * k + 8]
@@ -510,8 +534,10 @@
     for i, copy in enumerate(copies):
         copy.wait()
         done = done + ybox[i]
-    pos_out[...] = done[0:3]
-    vel_out[...] = done[3:6]
+    result[0:6, 0, :] = done[0:6]
+    last = pltpu.make_async_copy(result, out, load_sems.at[0])
+    last.start()
+    last.wait()
 
 
 def ring_coefficients():
@@ -529,18 +555,32 @@
     return table.reshape(NY, NY * 8, NZ * 8)
 
 
+def dmas(n):
+    return pltpu.SemaphoreType.DMA((n,))
+
+
+def like(x):
+    return pltpu.VMEM(x.shape, x.dtype)
+
+
 def finish_call(msgs, pos, vel, types, halo):
-    dma = lambda n: pltpu.SemaphoreType.DMA((n,))
     near = 2 * REACH
+    place = pl.BlockSpec(memory_space=PLACE)
     return pl.pallas_call(
         finish_kernel,
-        out_shape=(jax.ShapeDtypeStruct((3, LANES), F32),) * 3,
+        out_shape=jax.ShapeDtypeStruct((9, 1, LANES), F32),
+        in_specs=[place] * 6,
+        out_specs=place,
         scratch_shapes=[
+            pltpu.VMEM((8, LANES), F32),
+            like(pos), like(vel), like(types), like(halo),
+            pltpu.VMEM((NY * 8, NZ * 8), F32),
             pltpu.VMEM((7, 8, LANES), F32),
             pltpu.VMEM((NZ, 8, LANES), F32),
             pltpu.VMEM((NY, 8, LANES), F32),
             pltpu.VMEM((NY - 1, 8, LANES), F32),
-            dma(7), dma(7), dma(near), dma(near), dma(2), dma(2), dma(NY - 1), dma(NY - 1),
+            pltpu.VMEM((9, 1, LANES), F32),
+            dmas(7), dmas(7), dmas(near), dmas(near), dmas(2), dmas(2), dmas(NY - 1), dmas(NY - 1), dmas(6),
         ],
         compiler_params=pltpu.CompilerParams(collective_id=1, has_side_effects=True),
         name="finish",
@@ -553,35 +593,40 @@
     fit_first, fit_bias_first, fit_second, fit_bias_second, fit_third, fit_bias_third, fit_readout,
 ):
     del live_atoms
-    pos, vel, types = positions[:, 0, :], velocities[:, 0, :], atom_types[None]
+    types = atom_types[None]
     s1, a2, p1, a3, p2, _, _ = selections()
-    dma = lambda n: pltpu.SemaphoreType.DMA((n,))
-    vm = pl.BlockSpec(memory_space=pltpu.VMEM)
+    place = pl.BlockSpec(memory_space=PLACE)
+    weights = (
+        type_scale, type_shift, embed_two, embed_bias_two[None], embed_three, embed_bias_three[None],
+        jnp.asarray(s1), jnp.asarray(a2, BF16), jnp.asarray(p1, BF16), jnp.asarray(a3, BF16),
+        jnp.asarray(p2, BF16),
+    )
+    made = (
+        jax.ShapeDtypeStruct((56, 32), BF16),
+        jax.ShapeDtypeStruct((104, 56), BF16),
+        jax.ShapeDtypeStruct((4, 32, LANES), F32),
+    )
+    firsts = (positions, types, halo_rows)
     tiles, nb, w2t, w3t, cols = pl.pallas_call(
         exchange_kernel,
         out_shape=(
             jax.ShapeDtypeStruct((N_SLAB, 8, LANES), F32),
             jax.ShapeDtypeStruct((N_SLAB, SHARE, LANES), jnp.int32),
-            jax.ShapeDtypeStruct((56, 32), BF16),
-            jax.ShapeDtypeStruct((104, 56), BF16),
-            jax.ShapeDtypeStruct((4, 32, LANES), F32),
-        ),
-        in_specs=[vm] * 3 + [pl.BlockSpec(memory_space=pl.ANY)] + [vm] * 11,
-        out_specs=(vm,) * 5,
-        scratch_shapes=[dma(7), dma(7), dma(7), dma(7), pltpu.SemaphoreType.DMA],
+        ) + made,
+        in_specs=[place] * 15,
+        out_specs=(place,) * 5,
+        scratch_shapes=[like(x) for x in firsts + weights + made] + [
+            pltpu.VMEM((8, LANES), F32), dmas(7), dmas(7), dmas(7), dmas(7), dmas(5), dmas(14),
+        ],
         compiler_params=pltpu.CompilerParams(collective_id=0, has_side_effects=True),
         name="exchange",
-    )(
-        pos, types, halo_rows, neighbours.reshape(SHARE, N_SLAB, LANES), type_scale, type_shift,
-        embed_two, embed_bias_two[None], embed_three, embed_bias_three[None], jnp.asarray(s1),
-        jnp.asarray(a2, BF16), jnp.asarray(p1, BF16), jnp.asarray(a3, BF16), jnp.asarray(p2, BF16),
-    )
+    )(*firsts, neighbours.reshape(SHARE, N_SLAB, LANES), *weights)
     msgs = force_call(
         tiles, nb, w2t, w3t, cols,
         (fit_first, fit_bias_first, fit_second, fit_bias_second, fit_third, fit_bias_third, fit_readout),
     )
-    outs = finish_call(msgs, pos, vel, types, halo_rows)
-    return tuple(out[:, None, :] for out in outs)
+    out = finish_call(msgs, positions, velocities, types, halo_rows)
+    return out[0:3], out[3:6], out[6:9]
 
 
 def solution(mesh):

time: 57.9 us -> 51.5 us (0.89)
  the two profiles are of different devices: /device:TPU:1 before, /device:TPU:32 now
where the time goes in v3:
time: 51.5 us; the launch traced here: 51.1 us
  Pallas kernels  49.2 us (96%)
  local copies, waits for them, and re-layouts  1.25 us (2%)
  between operations  0.66 us (1%)
    pallas_call x1, Pallas kernels, finish_call(): pl.pallas_call(finish_kernel, out_shape=jax.ShapeDtypeStruct((9, 1, LANES...  30.7 us
    pallas_call x1, Pallas kernels, force_call(): pl.pallas_call(force_kernel, out_shape=jax.ShapeDtypeStruct((N_SLAB, 8, L...  10.8 us
    pallas_call x1, Pallas kernels, local(): pl.pallas_call(exchange_kernel, out_shape=(jax.ShapeDtypeStruct((N_SLAB,...  7.73 us
    slice x1, local copies, waits for them, and re-layouts, local(): return (out[0:3], out[3:6], out[6:9])  1.25 us

profile of v3, /device:TPU:32, one launch (start us, length us, event | category | flops | bytes accessed | tf_op | source)
XLA Modules:
  0.0 51.1 jit_solution(1901235081781096404)
XLA Ops:
  0.6 7.7 %exchange.1 = (f32[8,8,128]{2,1,0:T(8,128)}, s32[8,16,128]{2,1,0:T(8,128)}, bf16[56,32]{1,0:T(8,128)(2,1)}, bf16[104,56]{1,0:T(8,128)(2,1)}, f32[4,32,128]{2,1,0:T(8,128)}) custom-call(f32[3,1,128]{2,1,0:T(1,128)} %pos_in.1, s32[1,128]{1,0:T(1,128)} %bitcast.10, s32[1,128]{1,0:T(1,128)} %halo_in.1, s32[16,8,128]{2,1,0:T(8,128)} %bitcast.9, f32[2,25]{1,0:T(2,128)} %refs_4_.1, ...), custom_call_target="tpu_custom_call" | custom-call | tf_op jit(solution)/shard_map/exchange/pallas_call | solution.py:610
  8.4 10.8 %force.1.msgs = f32[8,8,128]{2,1,0:T(8,128)} custom-call(f32[8,8,128]{2,1,0:T(8,128)} %get-tuple-element.8.refs_0_, s32[8,16,128]{2,1,0:T(8,128)} %get-tuple-element.9.refs_1_, bf16[56,32]{1,0:T(8,128)(2,1)} %get-tuple-element.10.refs_2_, bf16[104,56]{1,0:T(8,128)(2,1)} %get-tuple-element.11.refs_3_, f32[4,32,128]{2,1,0:T(8,128)} %get-tuple-element.12.refs_4_, ...), custom_call_target="tpu_custom_call" | custom-call | tf_op jit(solution)/shard_map/force/pallas_call | solution.py:379
  19.1 30.7 %finish.1 = f32[9,1,128]{2,1,0:T(1,128)} custom-call(f32[8,8,128]{2,1,0:T(8,128)} %force.1.msgs, f32[3,1,128]{2,1,0:T(1,128)} %pos_in.1, f32[3,1,128]{2,1,0:T(1,128)} %vel_in.1, s32[1,128]{1,0:T(1,128)} %bitcast.11, s32[1,128]{1,0:T(1,128)} %halo_in.1, f32[4,32,128]{2,1,0:T(8,128)} %constant.23.clone.coefs_in), custom_call_target="tpu_custom_call" | custom-call | tf_op jit(solution)/shard_map/finish/pallas_call | solution.py:569
  49.8 1.3 %fusion = (f32[3,1,128]{2,1,0:T(1,128)}, f32[3,1,128]{2,1,0:T(1,128)}, f32[3,1,128]{2,1,0:T(1,128)}) fusion(f32[9,1,128]{2,1,0:T(1,128)} %finish.1), kind=kLoop, calls=%fused_computation | loop fusion | bytes 9216 | tf_op jit(solution)/shard_map/slice | solution.py:629

commit v4 on v3

--- a/solution.py
+++ b/solution.py
@@ -14,7 +14,9 @@
 LANES = 128
 STEP = 0.25
 HEAVY = 16.0
-BLK = 8
+BLK = 16
+BACK = 32
+MXU_GROUPS = 8
 CHUNK = 64
 F32 = jnp.float32
 BF16 = jnp.bfloat16
@@ -66,15 +68,14 @@
     b2 = np.zeros((50, 56), np.float32)
     for k in range(50):
         b2[two_feature(k), k] = 1
-    spread = np.full((16, LANES), 127, np.int32)
-    fold = np.zeros((13 * LANES, LANES), np.float32)
-    for g in range(13):
-        for lane in range(LANES):
-            e = 8 * g + lane // 16
-            spread[g, lane] = where[e]
-            if e < 100:
-                fold[g * LANES + lane, where[e]] = 1
-    return s1, a2, b1, a3, b2, spread, fold
+    fold = np.zeros((14 * LANES, LANES), np.float32)
+    places = np.full((16, LANES), 127, np.int32)
+    for lane in range(1600):
+        fold[lane, where[lane // 16]] = 1
+        places[lane // LANES, lane % LANES] = where[lane // 16]
+    for lane in range(LANES):
+        fold[13 * LANES + lane, lane % 16] = 1
+    return s1, a2, b1, a3, b2, places, fold
 
 
 def mode_matrices():
@@ -157,7 +158,7 @@
 def force_kernel(*refs):
     given, out, held, rest = refs[:14], refs[14], refs[15:29], refs[29:]
     (
-        tile, nb, w2t, w3t, cols, spread, c1, c2, c3, readout, fit1, fit2, fit3, fold,
+        tile, nb, w2t, w3t, cols, places, c1, c2, c3, readout, fit1, fit2, fit3, fold,
     ) = held
     env, geo, order, count, hc, three, feats, gfeats, qs, ps, scat, sems = rest
     me = lax.axis_index("slab")
@@ -176,7 +177,7 @@
         for j in range(SHARE):
             order[total + j] = s * SHARE + j
         total = total + count[s]
-    for j in range(BLK):
+    for j in range(max(BLK, BACK)):
         order[total + j] = N_SLAB * SHARE
     env[pl.ds(N_SLAB * SHARE * 8, 8), :] = jnp.zeros((8, LANES), F32)
 
@@ -249,17 +250,17 @@
             t = jnp.tanh(z[:, 256 * b : 256 * b + 128])
             d = (1.0 - t * t) * z[:, 256 * b + 128 : 256 * b + 256]
             two.append((
-                t + jnp.concatenate([t1[:24], t1[:24], t1[24:]], axis=0),
-                d + jnp.concatenate([d1[:24], d1[:24], d1[24:]], axis=0),
+                (t + jnp.concatenate([t1[:24], t1[:24], t1[24:]], axis=0)).astype(BF16),
+                (d + jnp.concatenate([d1[:24], d1[:24], d1[24:]], axis=0)).astype(BF16),
             ))
-        x = jnp.concatenate([a.astype(BF16) for pair in two for a in pair], axis=1)
+        x = jnp.concatenate([a for pair in two for a in pair], axis=1)
         z = dot(w3t[...], x, NN)
         for b in range(BLK):
             t2, d2 = two[b]
-            t = jnp.tanh(z[:, 256 * b : 256 * b + 128])
-            d = (1.0 - t * t) * z[:, 256 * b + 128 : 256 * b + 256]
-            l3 = (t + jnp.concatenate([t2[:48], t2[:48], t2[48:]], axis=0)).astype(BF16)
-            d3 = (d + jnp.concatenate([d2[:48], d2[:48], d2[48:]], axis=0)).astype(BF16)
+            t = jnp.tanh(z[:, 256 * b : 256 * b + 128].astype(BF16))
+            d = (1 - t * t) * z[:, 256 * b + 128 : 256 * b + 256].astype(BF16)
+            l3 = t + jnp.concatenate([t2[:48], t2[:48], t2[48:]], axis=0)
+            d3 = d + jnp.concatenate([d2[:48], d2[:48], d2[48:]], axis=0)
             three[first + b] = jnp.concatenate([l3, d3], axis=1)
             f = dot(e[b].astype(BF16), l3, NT) * (1.0 / 128.0)
             feats[pl.ds(pl.multiple_of((first + b) * 8, 8), 8), :] = jnp.concatenate(
@@ -278,12 +279,17 @@
     def fit(chunk, carry):
         base = chunk * (CHUNK * 8)
         fs = [feats[pl.ds(base + c, CHUNK, stride=8), :] for c in range(4)]
+        stack = jnp.concatenate(fs, axis=0).astype(BF16)
+        picks = dot(stack, fold[: MXU_GROUPS * LANES], NT)
         tiled = [lanes_of(f, lane_m & 15) for f in fs]
         spreads = [
-            [lanes_of(f, spread_rows(spread[g : g + 1, :], CHUNK)) for f in fs] for g in range(13)
+            [picks[CHUNK * c : CHUNK * (c + 1), g * LANES : (g + 1) * LANES] for g in range(MXU_GROUPS)]
+            + [lanes_of(fs[c], spread_rows(places[g : g + 1, :], CHUNK)) for g in range(MXU_GROUPS, 13)]
+            for c in range(4)
         ]
-        desc = [sum(spreads[g][c] * tiled[c] for c in range(4)) for g in range(13)]
-        desc = jnp.concatenate(desc, axis=1).astype(BF16)[:, :1600]
+        desc = [sum(spreads[c][g] * tiled[c] for c in range(4)).astype(BF16) for g in range(13)]
+        desc = jnp.concatenate(desc, axis=1)[:, :1600]
+        short = [v.astype(BF16) for v in tiled]
         f1 = jnp.tanh(dot(desc, fit1[...], NT) + c1[...])
         t2 = jnp.tanh(dot(f1.astype(BF16), fit2[...], NN) + c2[...])
         f2 = t2 + f1
@@ -296,21 +302,20 @@
         gd = dot((g1 * (1.0 - f1 * f1)).astype(BF16), fit1[...], NN)
         gd = jnp.concatenate([gd, jnp.zeros((CHUNK, 64), F32)], axis=1)
         parts = [gd[:, g * LANES : (g + 1) * LANES] for g in range(13)]
+        left = [jnp.concatenate([p.astype(BF16) * v for p in parts], axis=1) for v in short]
+        gf = dot(jnp.concatenate(left, axis=0), fold[: 13 * LANES], NN)
+        right = [sum(parts[g] * spreads[c][g] for g in range(13)) for c in range(4)]
+        gf = gf + dot(jnp.concatenate(right, axis=0).astype(BF16), fold[13 * LANES :], NN)
         for c in range(4):
-            left = jnp.concatenate([p * tiled[c] for p in parts], axis=1).astype(BF16)
-            left = dot(left, fold[...], NN)
-            right = sum(parts[g] * spreads[g][c] for g in range(13))
-            for shift in (64, 32, 16):
-                right = right + pltpu.roll(right, shift, 1)
-            gf = left + jnp.where(lane_m < 16, right, 0.0)
-            gfeats[pl.ds(base + c, CHUNK, stride=8), :] = gf * (1.0 / 128.0)
+            part = gf[CHUNK * c : CHUNK * (c + 1)] * (1.0 / 128.0)
+            gfeats[pl.ds(base + c, CHUNK, stride=8), :] = part
         return carry
 
     lax.fori_loop(0, lax.div(total + (CHUNK - 1), CHUNK), fit, 0)
 
     def back(block, carry):
-        first = block * BLK
-        for b in range(BLK):
+        first = block * BACK
+        for b in range(BACK):
             row = order[first + b]
             gf = gfeats[pl.ds(pl.multiple_of((first + b) * 8, 8), 8), :][:, :104]
             qp = dot(gf.astype(BF16), three[first + b], NN)
@@ -319,9 +324,9 @@
             ps[at, :] = qp[:, 128:]
         return carry
 
-    lax.fori_loop(0, blocks, back, 0)
-
-    sub = lax.broadcasted_iota(jnp.int32, (LANES, LANES), 0)
+    lax.fori_loop(0, lax.div(total + (BACK - 1), BACK), back, 0)
+
+    sub = lax.broadcasted_iota(jnp.int32, (LANES, LANES), 0).astype(F32).astype(BF16)
 
     def scatter(s, half):
         base = s * SHARE + half * 8
@@ -352,7 +357,8 @@
         for j in range(8):
             lhs.append(scat[pl.ds((base + j) * 8, 8), :].astype(BF16))
             low = nb[s, half * 8 + j : half * 8 + j + 1, :] & 127
-            rhs.append(jnp.where(sub == low, 1.0, 0.0).astype(BF16))
+            low = spread_rows(low.astype(F32).astype(BF16), LANES)
+            rhs.append(jnp.where(sub == low, jnp.ones_like(sub), jnp.zeros_like(sub)))
         grad = grad + dot(jnp.concatenate(lhs, axis=1), jnp.concatenate(rhs, axis=1), NT)
         if half == 0:
             feats[pl.ds(s * 8, 8), :] = grad
@@ -370,10 +376,10 @@
 
 def force_call(tile, nb, w2t, w3t, cols, fit):
     fit1, b1, fit2, b2, fit3, b3, readout = fit
-    _, _, _, _, _, spread, fold = selections()
+    places, fold = selections()[-2:]
     rows = N_SLAB * SHARE
     operands = (
-        tile, nb, w2t, w3t, cols, jnp.asarray(spread), b1[None], b2[None], b3[None], readout,
+        tile, nb, w2t, w3t, cols, jnp.asarray(places), b1[None], b2[None], b3[None], readout,
         fit1.T, fit2, fit3, jnp.asarray(fold, BF16),
     )
     return pl.pallas_call(
@@ -384,12 +390,12 @@
         scratch_shapes=[pltpu.VMEM(x.shape, x.dtype) for x in operands] + [
             pltpu.VMEM(((rows + 1) * 8, LANES), F32),
             pltpu.VMEM((5, rows, LANES), F32),
-            pltpu.SMEM((rows + 24,), jnp.int32),
+            pltpu.SMEM((rows + 48,), jnp.int32),
             pltpu.SMEM((N_SLAB,), jnp.int32),
-            pltpu.VMEM((rows + 8, LANES), F32),
-            pltpu.VMEM((rows + 8, 104, 256), BF16),
-            pltpu.VMEM(((rows + 8) * 8, LANES), F32),
-            pltpu.VMEM(((rows + 8) * 8, LANES), F32),
+            pltpu.VMEM((rows + 32, LANES), F32),
+            pltpu.VMEM((rows + 32, 104, 256), BF16),
+            pltpu.VMEM(((rows + 32) * 8, LANES), F32),
+            pltpu.VMEM(((rows + 32) * 8, LANES), F32),
             pltpu.VMEM(((rows + 1) * 8, LANES), F32),
             pltpu.VMEM(((rows + 1) * 8, LANES), F32),
             pltpu.VMEM((rows * 8, LANES), F32),
@@ -458,8 +464,8 @@
 
 def finish_kernel(
     msgs, pos_in, vel_in, types_in, halo_in, coefs_in, out,
-    mine, pos, vel, types, halo, coefs, inbox, ring, mixed, ybox, result,
-    slab_out, slab_in, ring_out, ring_in, far_out, far_in, y_out, y_in, load_sems,
+    mine, pos, vel, types, halo, coefs, inbox, ring, mixed, box, result,
+    slab_out, slab_in, ring_out, ring_in, last_out, last_in, load_sems,
 ):
     me, peers = slab_peers()
     bead = lax.axis_index("bead")
@@ -469,8 +475,7 @@
         return {"bead": lax.rem(z + NZ + d, NZ) * NY + y}
 
     steps = [d for k in range(1, REACH + 1) for d in (k, -k)]
-    yet = [lax.rem(y + k, NY) for k in range(1, NY)]
-    ypeers = [{"bead": z * NY + other} for other in yet]
+    ypeers = [{"bead": z * NY + lax.rem(y + k, NY)} for k in range(1, NY)]
     everyone = [along(d) for d in steps[::-1]] + peers + ypeers
     hail(everyone)
     loads = fetch(
@@ -497,62 +502,52 @@
     back = lax.dot_general(got, hit, NT, preferred_element_type=F32, precision=HIGH)
     force = -(got[0:3] + back[3:6])
     kicked = vel[:, 0, :] + STEP * jnp.where(types[...] == 1, 1.0, 1.0 / HEAVY) * force
-    own = ring.at[8]
+    own = ring.at[REACH]
     own[...] = jnp.concatenate([pos[:, 0, :], kicked, jnp.zeros((2, LANES), F32)], axis=0)
 
     near = {
-        d: send(own, ring.at[8 - d], ring_out.at[n], ring_in.at[n], along(d)) for n, d in enumerate(steps)
+        d: send(own, ring.at[REACH - d], ring_out.at[n], ring_in.at[n], along(d)) for n, d in enumerate(steps)
     }
     result[6:9, 0, :] = force
     for d in steps:
-        if d > 0:
-            near[d].wait_recv()
-    up = send(ring.at[pl.ds(4, 4)], ring.at[pl.ds(0, 4)], far_out.at[0], far_in.at[0], along(REACH))
-    for d in steps:
-        if d < 0:
-            near[d].wait_recv()
-    down = send(ring.at[pl.ds(9, 3)], ring.at[pl.ds(13, 3)], far_out.at[1], far_in.at[1], along(-REACH))
-    NN = (((1,), (0,)), ((), ()))
-    dot = functools.partial(lax.dot_general, preferred_element_type=F32, precision=HIGH)
-    table = coefs[...]
-    sums = dot(table[:, 32:104], jnp.concatenate([ring[n] for n in range(4, 13)], axis=0), NN)
-    for d in steps:
-        near[d].wait_send()
-    up.wait()
-    down.wait()
-    rest = [ring[n] for n in (0, 1, 2, 3, 13, 14, 15)]
-    sums = sums + dot(
-        jnp.concatenate([table[:, :32], table[:, 104:]], axis=1), jnp.concatenate(rest, axis=0), NN
-    )
-    for k in range(NY):
-        mixed[k] = sums[8 * k : 8 * k + 8]
-    copies = [
-        send(mixed.at[other], ybox.at[i], y_out.at[i], y_in.at[i], peer)
-        for i, (other, peer) in enumerate(zip(yet, ypeers))
-    ]
-    done = mixed[y]
-    for i, copy in enumerate(copies):
+        near[d].wait()
+    blocks = jnp.concatenate([ring[n] for n in range(2 * REACH + 1)], axis=0)
+    sums = lax.dot_general(
+        coefs[...], blocks, (((1,), (0,)), ((), ())), preferred_element_type=F32, precision=HIGH
+    )
+    copies = []
+    for n, (far, k) in enumerate(TARGETS):
+        if n != OWN:
+            mixed[n] = sums[8 * n : 8 * n + 8]
+            peer = {"bead": lax.rem(z + NZ + REACH * far, NZ) * NY + lax.rem(y + k, NY)}
+            copies.append((n, send(mixed.at[n], box.at[n], last_out.at[n], last_in.at[n], peer)))
+    done = sums[8 * OWN : 8 * OWN + 8]
+    for n, copy in copies:
         copy.wait()
-        done = done + ybox[i]
+        done = done + box[n]
     result[0:6, 0, :] = done[0:6]
-    last = pltpu.make_async_copy(result, out, load_sems.at[0])
-    last.start()
-    last.wait()
+    for load in fetch([(result, out)], load_sems):
+        load.wait()
+
+
+TARGETS = [(far, k) for far in (1, 0, -1) for k in range(NY)]
+OWN = TARGETS.index((0, 0))
 
 
 def ring_coefficients():
     cos, travel, spring = (m[:, 0].astype(np.float64) for m in mode_matrices())
-    table = np.zeros((NY, NY, 8, NZ, 8), np.float32)
+    table = np.zeros((NY, 3 * NY, 8, 2 * REACH + 1, 8), np.float32)
+    held = {1: range(-REACH, 0), 0: range(-REACH, REACH + 1), -1: range(1, REACH)}
     for y in range(NY):
-        for to in range(NY):
-            for slot in range(NZ):
-                apart = (to - y - NY * (slot - 8)) % BEADS
+        for n, (far, k) in enumerate(TARGETS):
+            for r in held[far]:
+                apart = (NY * (REACH * far - r) + (y + k) % NY - y) % BEADS
                 for c in range(3):
-                    table[y, to, c, slot, c] = cos[apart]
-                    table[y, to, c, slot, 3 + c] = travel[apart]
-                    table[y, to, 3 + c, slot, c] = -spring[apart]
-                    table[y, to, 3 + c, slot, 3 + c] = cos[apart]
-    return table.reshape(NY, NY * 8, NZ * 8)
+                    table[y, n, c, r + REACH, c] = cos[apart]
+                    table[y, n, c, r + REACH, 3 + c] = travel[apart]
+                    table[y, n, 3 + c, r + REACH, c] = -spring[apart]
+                    table[y, n, 3 + c, r + REACH, 3 + c] = cos[apart]
+    return table.reshape(NY, 3 * NY * 8, (2 * REACH + 1) * 8)
 
 
 def dmas(n):
@@ -574,13 +569,13 @@
         scratch_shapes=[
             pltpu.VMEM((8, LANES), F32),
             like(pos), like(vel), like(types), like(halo),
-            pltpu.VMEM((NY * 8, NZ * 8), F32),
+            pltpu.VMEM((3 * NY * 8, (near + 1) * 8), F32),
             pltpu.VMEM((7, 8, LANES), F32),
-            pltpu.VMEM((NZ, 8, LANES), F32),
-            pltpu.VMEM((NY, 8, LANES), F32),
-            pltpu.VMEM((NY - 1, 8, LANES), F32),
+            pltpu.VMEM((near + 1, 8, LANES), F32),
+            pltpu.VMEM((3 * NY, 8, LANES), F32),
+            pltpu.VMEM((3 * NY, 8, LANES), F32),
             pltpu.VMEM((9, 1, LANES), F32),
-            dmas(7), dmas(7), dmas(near), dmas(near), dmas(2), dmas(2), dmas(NY - 1), dmas(NY - 1), dmas(6),
+            dmas(7), dmas(7), dmas(near), dmas(near), dmas(3 * NY), dmas(3 * NY), dmas(6),
         ],
         compiler_params=pltpu.CompilerParams(collective_id=1, has_side_effects=True),
         name="finish",

time: 51.5 us -> 47.7 us (0.926)
  the two profiles are of different devices: /device:TPU:32 before, /device:TPU:1 now
where the time goes in v4:
time: 47.7 us; the launch traced here: 47.4 us
  Pallas kernels  45.5 us (95%)
  local copies, waits for them, and re-layouts  1.25 us (3%)
  between operations  0.66 us (1%)
    pallas_call x1, Pallas kernels, finish_call(): pl.pallas_call(finish_kernel, out_shape=jax.ShapeDtypeStruct((9, 1, LANES...  23 us
    pallas_call x1, Pallas kernels, local(): pl.pallas_call(exchange_kernel, out_shape=(jax.ShapeDtypeStruct((N_SLAB,...  13.5 us
    pallas_call x1, Pallas kernels, force_call(): pl.pallas_call(force_kernel, out_shape=jax.ShapeDtypeStruct((N_SLAB, 8, L...  8.98 us
    slice x1, local copies, waits for them, and re-layouts, local(): return (out[0:3], out[3:6], out[6:9])  1.25 us

profile of v4, /device:TPU:1, one launch (start us, length us, event | category | flops | bytes accessed | tf_op | source)
XLA Modules:
  0.0 47.4 jit_solution(15507820114665917203)
XLA Ops:
  0.6 13.5 %exchange.1 = (f32[8,8,128]{2,1,0:T(8,128)}, s32[8,16,128]{2,1,0:T(8,128)}, bf16[56,32]{1,0:T(8,128)(2,1)}, bf16[104,56]{1,0:T(8,128)(2,1)}, f32[4,32,128]{2,1,0:T(8,128)}) custom-call(f32[3,1,128]{2,1,0:T(1,128)} %pos_in.1, s32[1,128]{1,0:T(1,128)} %bitcast.10, s32[1,128]{1,0:T(1,128)} %halo_in.1, s32[16,8,128]{2,1,0:T(8,128)} %bitcast.9, f32[2,25]{1,0:T(2,128)} %refs_4_.1, ...), custom_call_target="tpu_custom_call" | custom-call | tf_op jit(solution)/shard_map/exchange/pallas_call | solution.py:605
  14.1 9.0 %force.1.msgs = f32[8,8,128]{2,1,0:T(8,128)} custom-call(f32[8,8,128]{2,1,0:T(8,128)} %get-tuple-element.8.refs_0_, s32[8,16,128]{2,1,0:T(8,128)} %get-tuple-element.9.refs_1_, bf16[56,32]{1,0:T(8,128)(2,1)} %get-tuple-element.10.refs_2_, bf16[104,56]{1,0:T(8,128)(2,1)} %get-tuple-element.11.refs_3_, f32[4,32,128]{2,1,0:T(8,128)} %get-tuple-element.12.refs_4_, ...), custom_call_target="tpu_custom_call" | custom-call | tf_op jit(solution)/shard_map/force/pallas_call | solution.py:385
  23.1 23.0 %finish.1 = f32[9,1,128]{2,1,0:T(1,128)} custom-call(f32[8,8,128]{2,1,0:T(8,128)} %force.1.msgs, f32[3,1,128]{2,1,0:T(1,128)} %pos_in.1, f32[3,1,128]{2,1,0:T(1,128)} %vel_in.1, s32[1,128]{1,0:T(1,128)} %bitcast.11, s32[1,128]{1,0:T(1,128)} %halo_in.1, f32[4,96,72]{2,1,0:T(8,128)} %constant.23.clone.coefs_in), custom_call_target="tpu_custom_call" | custom-call | tf_op jit(solution)/shard_map/finish/pallas_call | solution.py:564
  46.1 1.3 %fusion = (f32[3,1,128]{2,1,0:T(1,128)}, f32[3,1,128]{2,1,0:T(1,128)}, f32[3,1,128]{2,1,0:T(1,128)}) fusion(f32[9,1,128]{2,1,0:T(1,128)} %finish.1), kind=kLoop, calls=%fused_computation | loop fusion | bytes 9216 | tf_op jit(solution)/shard_map/slice | solution.py:624

commit v5 on v4

--- a/solution.py
+++ b/solution.py
@@ -230,10 +230,9 @@
         load.wait()
     sc0, sc1, sh0, sh1 = 0, 1, 2, 3
 
-    def forward(block, carry):
-        first = block * BLK
+    def forward(first, size):
         e, one, done = [], [], []
-        for b in range(BLK):
+        for b in range(size):
             row = order[first + b]
             v = env[pl.ds(pl.multiple_of(row * 8, 8), 8), :]
             e.append(v)
@@ -245,7 +244,7 @@
         x = jnp.concatenate([a.astype(BF16) for pair in one for a in pair], axis=1)
         z = dot(w2t[...], x, NN)
         two = []
-        for b in range(BLK):
+        for b in range(size):
             t1, d1 = one[b]
             t = jnp.tanh(z[:, 256 * b : 256 * b + 128])
             d = (1.0 - t * t) * z[:, 256 * b + 128 : 256 * b + 256]
@@ -255,7 +254,7 @@
             ))
         x = jnp.concatenate([a for pair in two for a in pair], axis=1)
         z = dot(w3t[...], x, NN)
-        for b in range(BLK):
+        for b in range(size):
             t2, d2 = two[b]
             t = jnp.tanh(z[:, 256 * b : 256 * b + 128].astype(BF16))
             d = (1 - t * t) * z[:, 256 * b + 128 : 256 * b + 256].astype(BF16)
@@ -266,10 +265,19 @@
             feats[pl.ds(pl.multiple_of((first + b) * 8, 8), 8), :] = jnp.concatenate(
                 [f, jnp.zeros((8, 24), F32)], axis=1
             )
+
+    full = lax.div(total + (BLK // 2 - 1), BLK)
+
+    def whole_step(block, carry):
+        forward(block * BLK, BLK)
         return carry
 
-    blocks = lax.div(total + (BLK - 1), BLK)
-    lax.fori_loop(0, blocks, forward, 0)
+    def half_step(block, carry):
+        forward(full * BLK, BLK // 2)
+        return carry
+
+    lax.fori_loop(0, full, whole_step, 0)
+    lax.fori_loop(0, jnp.where(total > full * BLK, 1, 0), half_step, 0)
 
     for load in loads[6:]:
         load.wait()
@@ -462,6 +470,11 @@
         copy.wait()
 
 
+def halves(x):
+    high = x.astype(BF16)
+    return high, (x - high.astype(F32)).astype(BF16)
+
+
 def finish_kernel(
     msgs, pos_in, vel_in, types_in, halo_in, coefs_in, out,
     mine, pos, vel, types, halo, coefs, inbox, ring, mixed, box, result,
@@ -474,9 +487,10 @@
     def along(d):
         return {"bead": lax.rem(z + NZ + d, NZ) * NY + y}
 
-    steps = [d for k in range(1, REACH + 1) for d in (k, -k)]
+    steps = [d for k in range(REACH, 0, -1) for d in (k, -k)]
+    used = pl.ds(0, 6)
     ypeers = [{"bead": z * NY + lax.rem(y + k, NY)} for k in range(1, NY)]
-    everyone = [along(d) for d in steps[::-1]] + peers + ypeers
+    everyone = [along(d) for d in steps] + peers + ypeers
     hail(everyone)
     loads = fetch(
         [
@@ -488,22 +502,24 @@
     for load in loads:
         load.wait()
     bins = pltpu.roll(spread_rows(halo[...], 8), 64, 1)[0:1]
-    hit = jnp.where(lax.broadcasted_iota(jnp.int32, (LANES, LANES), 0) == bins, 1.0, 0.0)
+    hit = jnp.where(lax.broadcasted_iota(jnp.int32, (LANES, LANES), 0) == bins, 1.0, 0.0).astype(BF16)
     meet(everyone)
 
     copies = [
-        send(msgs.at[lax.rem(me + i + 1, N_SLAB)], inbox.at[i], slab_out.at[i], slab_in.at[i], peer)
+        send(msgs.at[lax.rem(me + i + 1, N_SLAB), used], inbox.at[i], slab_out.at[i], slab_in.at[i], peer)
         for i, peer in enumerate(peers)
     ]
-    got = mine[...]
+    got = mine[0:6, :]
     for i, copy in enumerate(copies):
         copy.wait()
         got = got + inbox[i]
-    back = lax.dot_general(got, hit, NT, preferred_element_type=F32, precision=HIGH)
+    high, low = halves(got)
+    dot = functools.partial(lax.dot_general, preferred_element_type=F32)
+    back = dot(high, hit, NT) + dot(low, hit, NT)
     force = -(got[0:3] + back[3:6])
     kicked = vel[:, 0, :] + STEP * jnp.where(types[...] == 1, 1.0, 1.0 / HEAVY) * force
     own = ring.at[REACH]
-    own[...] = jnp.concatenate([pos[:, 0, :], kicked, jnp.zeros((2, LANES), F32)], axis=0)
+    own[...] = jnp.concatenate([pos[:, 0, :], kicked], axis=0)
 
     near = {
         d: send(own, ring.at[REACH - d], ring_out.at[n], ring_in.at[n], along(d)) for n, d in enumerate(steps)
@@ -511,26 +527,26 @@
     result[6:9, 0, :] = force
     for d in steps:
         near[d].wait()
-    blocks = jnp.concatenate([ring[n] for n in range(2 * REACH + 1)], axis=0)
-    sums = lax.dot_general(
-        coefs[...], blocks, (((1,), (0,)), ((), ())), preferred_element_type=F32, precision=HIGH
-    )
+    blank = jnp.zeros((2, LANES), F32)
+    blocks = [x for n in range(2 * REACH + 1) for x in (ring[n], blank)] + [jnp.zeros((8, LANES), F32)]
+    high, low = halves(jnp.concatenate(blocks, axis=0))
+    sums = dot(coefs[...], jnp.concatenate([high, high, low], axis=0), (((1,), (0,)), ((), ())))
     copies = []
     for n, (far, k) in enumerate(TARGETS):
         if n != OWN:
-            mixed[n] = sums[8 * n : 8 * n + 8]
+            mixed[n] = sums[8 * n : 8 * n + 6]
             peer = {"bead": lax.rem(z + NZ + REACH * far, NZ) * NY + lax.rem(y + k, NY)}
             copies.append((n, send(mixed.at[n], box.at[n], last_out.at[n], last_in.at[n], peer)))
-    done = sums[8 * OWN : 8 * OWN + 8]
+    done = sums[8 * OWN : 8 * OWN + 6]
     for n, copy in copies:
         copy.wait()
         done = done + box[n]
-    result[0:6, 0, :] = done[0:6]
+    result[0:6, 0, :] = done
     for load in fetch([(result, out)], load_sems):
         load.wait()
 
 
-TARGETS = [(far, k) for far in (1, 0, -1) for k in range(NY)]
+TARGETS = [(far, k) for k in (2, 1, 3, 0) for far in (1, -1)] + [(0, k) for k in (2, 1, 3, 0)]
 OWN = TARGETS.index((0, 0))
 
 
@@ -547,7 +563,11 @@
                     table[y, n, c, r + REACH, 3 + c] = travel[apart]
                     table[y, n, 3 + c, r + REACH, c] = -spring[apart]
                     table[y, n, 3 + c, r + REACH, 3 + c] = cos[apart]
-    return table.reshape(NY, 3 * NY * 8, (2 * REACH + 1) * 8)
+    table = table.reshape(NY, 3 * NY * 8, (2 * REACH + 1) * 8)
+    table = np.pad(table, ((0, 0), (0, 0), (0, 8)))
+    high = table.astype(jnp.bfloat16)
+    low = (table - high.astype(np.float32)).astype(jnp.bfloat16)
+    return np.concatenate([high, low, high], axis=2)
 
 
 def dmas(n):
@@ -569,11 +589,11 @@
         scratch_shapes=[
             pltpu.VMEM((8, LANES), F32),
             like(pos), like(vel), like(types), like(halo),
-            pltpu.VMEM((3 * NY * 8, (near + 1) * 8), F32),
-            pltpu.VMEM((7, 8, LANES), F32),
-            pltpu.VMEM((near + 1, 8, LANES), F32),
-            pltpu.VMEM((3 * NY, 8, LANES), F32),
-            pltpu.VMEM((3 * NY, 8, LANES), F32),
+            pltpu.VMEM((3 * NY * 8, 3 * (near + 2) * 8), BF16),
+            pltpu.VMEM((7, 6, LANES), F32),
+            pltpu.VMEM((near + 1, 6, LANES), F32),
+            pltpu.VMEM((3 * NY, 6, LANES), F32),
+            pltpu.VMEM((3 * NY, 6, LANES), F32),
             pltpu.VMEM((9, 1, LANES), F32),
             dmas(7), dmas(7), dmas(near), dmas(near), dmas(3 * NY), dmas(3 * NY), dmas(6),
         ],

time: 47.7 us -> 46.8 us (0.981)
  Pallas kernels: 45.5 us -> 44.3 us
    pallas_call x1, Pallas kernels: 8.98 us -> 8.02 us  [force_call(): pl.pallas_call(force_kernel, out_shape=jax.ShapeDtypeStruct((N_SLAB, 8, L...]
where the time goes in v5:
time: 46.8 us; the launch traced here: 46.2 us
  Pallas kernels  44.3 us (95%)
  local copies, waits for them, and re-layouts  1.25 us (3%)
  between operations  0.66 us (1%)
    pallas_call x1, Pallas kernels, finish_call(): pl.pallas_call(finish_kernel, out_shape=jax.ShapeDtypeStruct((9, 1, LANES...  22.8 us
    pallas_call x1, Pallas kernels, local(): pl.pallas_call(exchange_kernel, out_shape=(jax.ShapeDtypeStruct((N_SLAB,...  13.5 us
    pallas_call x1, Pallas kernels, force_call(): pl.pallas_call(force_kernel, out_shape=jax.ShapeDtypeStruct((N_SLAB, 8, L...  8.02 us
    slice x1, local copies, waits for them, and re-layouts, local(): return (out[0:3], out[3:6], out[6:9])  1.25 us

profile of v5, /device:TPU:1, one launch (start us, length us, event | category | flops | bytes accessed | tf_op | source)
XLA Modules:
  0.0 46.2 jit_solution(6995834463723518524)
XLA Ops:
  0.6 13.5 %exchange.1 = (f32[8,8,128]{2,1,0:T(8,128)}, s32[8,16,128]{2,1,0:T(8,128)}, bf16[56,32]{1,0:T(8,128)(2,1)}, bf16[104,56]{1,0:T(8,128)(2,1)}, f32[4,32,128]{2,1,0:T(8,128)}) custom-call(f32[3,1,128]{2,1,0:T(1,128)} %pos_in.1, s32[1,128]{1,0:T(1,128)} %bitcast.10, s32[1,128]{1,0:T(1,128)} %halo_in.1, s32[16,8,128]{2,1,0:T(8,128)} %bitcast.9, f32[2,25]{1,0:T(2,128)} %refs_4_.1, ...), custom_call_target="tpu_custom_call" | custom-call | tf_op jit(solution)/shard_map/exchange/pallas_call | solution.py:625
  14.1 8.0 %force.1.msgs = f32[8,8,128]{2,1,0:T(8,128)} custom-call(f32[8,8,128]{2,1,0:T(8,128)} %get-tuple-element.8.refs_0_, s32[8,16,128]{2,1,0:T(8,128)} %get-tuple-element.9.refs_1_, bf16[56,32]{1,0:T(8,128)(2,1)} %get-tuple-element.10.refs_2_, bf16[104,56]{1,0:T(8,128)(2,1)} %get-tuple-element.11.refs_3_, f32[4,32,128]{2,1,0:T(8,128)} %get-tuple-element.12.refs_4_, ...), custom_call_target="tpu_custom_call" | custom-call | tf_op jit(solution)/shard_map/force/pallas_call | solution.py:393
  22.1 22.8 %finish.1 = f32[9,1,128]{2,1,0:T(1,128)} custom-call(f32[8,8,128]{2,1,0:T(8,128)} %force.1.msgs, f32[3,1,128]{2,1,0:T(1,128)} %pos_in.1, f32[3,1,128]{2,1,0:T(1,128)} %vel_in.1, s32[1,128]{1,0:T(1,128)} %bitcast.11, s32[1,128]{1,0:T(1,128)} %halo_in.1, bf16[4,96,240]{2,1,0:T(8,128)(2,1)} %constant.23.clone.coefs_in), custom_call_target="tpu_custom_call" | custom-call | tf_op jit(solution)/shard_map/finish/pallas_call | solution.py:584
  45.0 1.3 %fusion = (f32[3,1,128]{2,1,0:T(1,128)}, f32[3,1,128]{2,1,0:T(1,128)}, f32[3,1,128]{2,1,0:T(1,128)}) fusion(f32[9,1,128]{2,1,0:T(1,128)} %finish.1), kind=kLoop, calls=%fused_computation | loop fusion | bytes 9216 | tf_op jit(solution)/shard_map/slice | solution.py:644
